TPU v7x, 32 devices: a whole 2x2x4 slice. The times are simulated.
32 devices in a mesh: tm: 8 (over y, x, core), grp: 4 (over z).
Axes of the slice: x: 2, y: 2, z: 4, core: 2. Of those that a mesh axis runs over, the one named last changes fastest.
Arguments:
- series: float32 [131072, 512], P(('tm', 'grp')), may hold values from -6 to 6
- filter_taps: float32 [33], replicated, may hold values from -1 to 1
- sign_flips: int32 [131072], P(('tm', 'grp')), may hold values from -1 to 1, as said below
- samples: int32 [8192], replicated, may hold values from 0 to 131071, as said below
Outputs:
- sketch: float32 [8192, 512], P(('tm', 'grp'))
- r_factor: float32 [512, 512], replicated
Inputs may be any that keep to these rules, and one draw needn't show every extreme that they name: `sign_flips`: each entry is -1 or +1. All distinct; the values of samples modulo 4096 take exactly 4096 distinct values, each by exactly 2 consecutive entries; entries are ordered by their value modulo 4096, then by value.
All inputs are finite; a program needn't handle non-finite values.
Results may differ from a plain program's by a relative error of at most 0.0003.
Values sent between devices are 32-bit elements; how exact they have to be, the bound alone decides.
A program may use at most 128 MiB of HBM per device.

v0:
```python
import jax
import jax.numpy as jnp
from jax import lax
from jax.sharding import PartitionSpec as P


def extended(block, sides, width):
    for axis, dim in sides:
        count = lax.axis_size(axis)
        forward = [(i, i + 1) for i in range(count - 1)]
        backward = [(target, source) for source, target in forward]
        low = lax.ppermute(
            lax.slice_in_dim(block, block.shape[dim] - width, None, axis=dim), axis, forward
        )
        high = lax.ppermute(lax.slice_in_dim(block, 0, width, axis=dim), axis, backward)
        block = jnp.concatenate([low, block, high], axis=dim)
    return block


def bit_count(values, width_bits):
    counted = jnp.zeros_like(values)
    for offset in range(width_bits):
        counted = counted + (values >> offset & 1)
    return counted


def hadamard(order):
    row_ids = jnp.arange(order, dtype=jnp.int32)[:, None]
    col_ids = jnp.arange(order, dtype=jnp.int32)[None, :]
    parity = bit_count(row_ids & col_ids, max(order.bit_length(), 1)) & 1
    return (1 - 2 * parity).astype(jnp.float32)


def local_transform(rows_block):
    length, columns = rows_block.shape
    levels = length.bit_length() - 1
    outer = 2 ** ((levels + 1) // 2)
    inner = length // outer
    layered = rows_block.reshape(outer, inner, columns)
    layered = jnp.einsum("ux,xvw->uvw", hadamard(outer), layered, precision=lax.Precision.HIGHEST)
    layered = jnp.einsum("vy,uyw->uvw", hadamard(inner), layered, precision=lax.Precision.HIGHEST)
    return layered.reshape(length, columns)


def on_device(series, filter_taps, sign_flips, samples):
    rows_dev = series.shape[0]
    columns = series.shape[1]
    tap_count = filter_taps.shape[0]
    half_taps = (tap_count - 1) // 2
    devices_all = lax.axis_size("tm") * lax.axis_size("grp")
    total_rows = rows_dev * devices_all
    sample_count = samples.shape[0]
    padded = extended(series, ((("tm", "grp"), 0),), half_taps)
    filtered = filter_taps[0] * padded[0:rows_dev]
    for offset in range(1, tap_count):
        filtered = filtered + filter_taps[offset] * padded[offset : offset + rows_dev]
    flipped = filtered * sign_flips.astype(jnp.float32)[:, None]
    mixed = local_transform(flipped)
    position = lax.axis_index("tm") * lax.axis_size("grp") + lax.axis_index("grp")
    row_scale = 1.0 / jnp.sqrt(jnp.float32(total_rows))
    block_rows = sample_count // devices_all
    copies = max(2, sample_count // rows_dev)
    distinct = sample_count // copies
    per_device = distinct // devices_all
    used_positions = samples[::copies] % rows_dev
    outgoing = jnp.take(mixed, used_positions, axis=0)
    incoming = lax.all_to_all(outgoing, ("tm", "grp"), split_axis=0, concat_axis=0, tiled=True)
    stacked = incoming.reshape(devices_all, per_device, columns)
    combined = (
        jnp.einsum("op,pkw->okw", hadamard(devices_all), stacked, precision=lax.Precision.HIGHEST)
        * row_scale
    )
    combined = combined.reshape(devices_all * per_device, columns)
    mine = lax.dynamic_slice_in_dim(samples, position * block_rows, block_rows)
    slot_index = mine // rows_dev * per_device + jnp.arange(block_rows, dtype=jnp.int32) // copies
    sketch = jnp.take(combined, slot_index, axis=0)
    local_gram = lax.dot_general(
        sketch,
        sketch,
        (((0,), (0,)), ((), ())),
        precision=lax.Precision.HIGHEST,
        preferred_element_type=jnp.float32,
    )
    gram = lax.psum(local_gram, ("tm", "grp"))
    lower = jnp.linalg.cholesky(gram / sample_count)
    return (sketch, lower.T)


def solution(mesh):
    return jax.shard_map(
        on_device,
        mesh=mesh,
        in_specs=(P(("tm", "grp"), None), P(), P(("tm", "grp")), P()),
        out_specs=(P(("tm", "grp"), None), P()),
        check_vma=False,
    )
```

profile of v0, /device:TPU:0, one launch (start us, length us, event | category | flops | bytes accessed | tf_op | source)
XLA Modules:
  0.0 659.5 jit_solution(13701622514079241855)
XLA Ops:
  7.9 4.9 collective-permute-start
  15.6 2.1 fusion.111
  17.7 1.9 fusion.112
  20.9 11.5 %constant_dynamic-update-slice_fusion = (f32[4112,512]{1,0:T(8,128)}, f32[4112,512]{1,0:T(8,128)}) fusion(f32[4112,512]{1,0:T(8,128)} %constant_dynamic-update-slice_fusion.1, f32[4096,512]{1,0:T(8,128)} %param.4), kind=kLoop, calls=%fused_computation.143 | loop fusion | bytes 25165824 | tf_op jit(solution)/shard_map/concatenate | solution.py:16
  33.0 122.8 %fusion.1 = f32[4096,512]{1,0:T(8,128)S(1)} fusion(f32[4112,512]{1,0:T(8,128)} %constant_dynamic-update-slice_fusion.2, f32[4112,512]{1,0:T(8,128)} %get-tuple-element.10, f32[4096,512]{1,0:T(8,128)} %param.4, f32[4096]{0:T(1024)S(1)} %convert_element_type.14, f32[]{:T(128)} %bitcast.35, f32[]{:T(128)} %bitcast.34, f32[]{:T(128)} %bitcast.33, f32[]{:T(128)} %bitcast.32, ...), kind=kLoop, calls=%fused_computation.4 | loop fusion | flops 138412032 | bytes 285229184 | tf_op jit(solution)/shard_map/mul | solution.py:57
  155.8 12.4 %fusion.37 = f32[64,64,512]{2,0,1:T(8,128)S(1)} fusion(f32[64,64,512]{2,1,0:T(8,128)S(1)} %bitcast.77), kind=kOutput, calls=%fused_computation.71 | convolution fusion | flops 1610715136 | bytes 16777216 | tf_op jit(solution)/shard_map/ux,xvw->uvw/dot_general | solution.py:40
  168.3 13.8 %fusion.35 = f32[64,512,64]{1,2,0:T(8,128)} fusion(f32[64,64,512]{2,0,1:T(8,128)S(1)} %fusion.37), kind=kOutput, calls=%fused_computation.69 | convolution fusion | flops 1610715136 | bytes 16777216 | tf_op jit(solution)/shard_map/vy,uyw->uvw/dot_general | solution.py:41
  182.1 21.4 %gather_fusion = f32[4096,512]{1,0:T(8,128)} fusion(f32[4096,512]{1,0:T(8,128)} %bitcast.75, s32[4096]{0:T(1024)S(1)} %broadcast_clamp_fusion), kind=kCustom, calls=%fused_computation | custom fusion | bytes 16793600 | tf_op jit(solution)/shard_map/jit(_take)/gather | solution.py:66
  203.5 5.8 broadcast_select_fusion
  209.3 7.0 %all-to-all-start = ((f32[32,128,512]{2,1,0:T(8,128)}), f32[32,128,512]{2,1,0:T(8,128)}, u32[]{:S(2)}, u32[]{:S(2)}) async-start(f32[32,128,512]{2,1,0:T(8,128)} %broadcast_select_fusion), calls=%async_computation | async-start | bytes 16777216 | tf_op jit(solution)/shard_map/all_to_all | solution.py:67
  217.2 180.5 %all-to-all-done = f32[32,128,512]{2,1,0:T(8,128)} async-done(((f32[32,128,512]{2,1,0:T(8,128)}), f32[32,128,512]{2,1,0:T(8,128)}, u32[]{:S(2)}, u32[]{:S(2)}) %all-to-all-start) | async-done | bytes 8388640 | tf_op jit(solution)/shard_map/all_to_all | solution.py:67
  397.7 16.9 %broadcast_multiply_fusion = f32[32,128,512]{2,0,1:T(8,128)S(1)} fusion(f32[32,128,512]{2,1,0:T(8,128)} %all-to-all-done), kind=kOutput, calls=%fused_computation.73 | convolution fusion | flops 807426048 | bytes 16777216 | tf_op jit(solution)/shard_map/op,pkw->okw/dot_general | solution.py:70
  414.6 8.1 %copy.18 = f32[32,128,512]{2,1,0:T(8,128)} copy(f32[32,128,512]{2,0,1:T(8,128)S(1)} %broadcast_multiply_fusion) | data formatting | bytes 16777216 | tf_op jit(solution)/shard_map/mul | solution.py:70
  422.7 4.6 gather_fusion.1
  427.4 2.0 fusion.113
  429.4 134.7 %all-reduce.3.cloned.1.call-done = f32[512,512]{0,1:T(8,128)} async-done(((f32[512,512]{0,1:T(8,128)}), f32[512,512]{0,1:T(8,128)}) %all-reduce.3.cloned.1.call-update) | async-done | bytes 1048592 | tf_op jit(solution)/shard_map/psum | solution.py:84
  565.8 1.5 fusion.41
  567.3 11.7 %cholesky.104 = f32[128,128]{1,0:T(8,128)S(1)} custom-call(f32[128,128]{1,0:T(8,128)S(1)} %cholesky.266), custom_call_target="Cholesky" | custom-call | tf_op jit(solution)/shard_map/jit(cholesky)/cholesky | solution.py:85
  579.2 10.0 %custom-call.27 = f32[1,128,128]{1,2,0:T(8,128)S(1)} custom-call(f32[1,128,128]{2,1,0:T(8,128)S(1)} %get-tuple-element.23), custom_call_target="InvertDiagBlocksLowerTriangular" | custom-call | tf_op jit(solution)/shard_map/jit(cholesky)/cholesky | solution.py:85
  589.8 11.7 %cholesky.217 = f32[128,128]{1,0:T(8,128)S(1)} custom-call(f32[128,128]{1,0:T(8,128)S(1)} %cholesky.270), custom_call_target="Cholesky" | custom-call | tf_op jit(solution)/shard_map/jit(cholesky)/cholesky | solution.py:85
  601.6 9.8 %custom-call.28 = f32[1,128,128]{1,2,0:T(8,128)S(1)} custom-call(f32[1,128,128]{2,1,0:T(8,128)S(1)} %get-tuple-element.20), custom_call_target="InvertDiagBlocksLowerTriangular" | custom-call | tf_op jit(solution)/shard_map/jit(cholesky)/cholesky | solution.py:85
  612.1 11.9 %cholesky.238 = f32[128,128]{1,0:T(8,128)S(1)} custom-call(f32[128,128]{1,0:T(8,128)S(1)} %cholesky.275), custom_call_target="Cholesky" | custom-call | tf_op jit(solution)/shard_map/jit(cholesky)/cholesky | solution.py:85
  624.0 9.8 %custom-call.29 = f32[1,128,128]{1,2,0:T(8,128)S(1)} custom-call(f32[1,128,128]{2,1,0:T(8,128)S(1)} %get-tuple-element.17), custom_call_target="InvertDiagBlocksLowerTriangular" | custom-call | tf_op jit(solution)/shard_map/jit(cholesky)/cholesky | solution.py:85
  634.5 11.7 %cholesky.255 = f32[128,128]{1,0:T(8,128)S(1)} custom-call(f32[128,128]{1,0:T(8,128)S(1)} %convolution_subtract_fusion.2), custom_call_target="Cholesky" | custom-call | tf_op jit(solution)/shard_map/jit(cholesky)/cholesky | solution.py:85
  (38 shorter events, 13.6 us)
Async XLA Ops:
  7.9 12.4 %collective-permute-start = (f32[16,512]{1,0:T(8,128)S(1)}, f32[16,512]{1,0:T(8,128)S(1)}, u32[]{:S(2)}, u32[]{:S(2)}) collective-permute-start(f32[16,512]{1,0:T(8,128)S(1)} %get-tuple-element.12), channel_id=1, source_target_pairs={{0,1},{1,2},{2,3},{3,4},{4,5},{5,6},{6,7},{7,8},{8,9},{9,10},{10,1... | collective-permute-start | bytes 98312 | tf_op jit(solution)/shard_map/ppermute | solution.py:12
  12.9 19.5 %collective-permute-start.1 = (f32[16,512]{1,0:T(8,128)S(1)}, f32[16,512]{1,0:T(8,128)S(1)}, u32[]{:S(2)}, u32[]{:S(2)}) collective-permute-start(f32[16,512]{1,0:T(8,128)S(1)} %get-tuple-element.13), channel_id=1, source_target_pairs={{1,0},{2,1},{3,2},{4,3},{5,4},{6,5},{7,6},{8,7},{9,8},{10,9},{11,1... | collective-permute-start | bytes 98312 | tf_op jit(solution)/shard_map/ppermute | solution.py:15
  209.3 188.4 %all-to-all-start = ((f32[32,128,512]{2,1,0:T(8,128)}), f32[32,128,512]{2,1,0:T(8,128)}, u32[]{:S(2)}, u32[]{:S(2)}) async-start(f32[32,128,512]{2,1,0:T(8,128)} %broadcast_select_fusion), calls=%async_computation | async-start | bytes 16777216 | tf_op jit(solution)/shard_map/all_to_all | solution.py:67
  216.3 347.8 %all-reduce.3.cloned.1.call-start = ((), (), s32[]{:S(2)}) async-start(), calls=%async_computation.1 | async-start | bytes 2097152 | tf_op jit(solution)/shard_map/psum | solution.py:84
  427.4 223.5 %copy-start = (f32[256,512]{1,0:T(8,128)}, f32[256,512]{1,0:T(8,128)S(1)}, u32[]{:S(2)}) copy-start(f32[256,512]{1,0:T(8,128)S(1)} %broadcast_select_fusion.1) | copy-start | bytes 1572868
Sparse Core Ops, SparseCore 0:
  429.5 134.5 all-reduce.2
where the time goes:
time: 664 us; the launch traced here: 659 us
  waiting for transfers between devices  315 us (47%)
  other arithmetic  212 us (32%)
  local copies, waits for them, and re-layouts  54.7 us (8%)
  matrix products  47 us (7%)
  between operations  17.3 us (3%)
  starting transfers between devices  13.3 us (2%)
    all_to_all x1, waiting for transfers between devices, on_device(): lax.all_to_all(outgoing, ('tm', 'grp'), split_axis=0, concat_axis=0, tile...  181 us
    psum x1, waiting for transfers between devices, on_device(): gram = lax.psum(local_gram, ('tm', 'grp'))  135 us
    mul x1, other arithmetic, on_device(): flipped = filtered * sign_flips.astype(jnp.float32)[:, None]  123 us
    another operation x14, other arithmetic, on_device(): lower = jnp.linalg.cholesky(gram / sample_count)  78.8 us
    gather x1, local copies, waits for them, and re-layouts, on_device(): outgoing = jnp.take(mixed, used_positions, axis=0)  21.4 us
    dot_general x1, matrix products, on_device(): jnp.einsum('op,pkw->okw', hadamard(devices_all), stacked, precision=lax.P...  16.9 us
    dot_general x1, matrix products, local_transform(): jnp.einsum('vy,uyw->uvw', hadamard(inner), layered, precision=lax.Precisi...  13.8 us
  transfers between devices with their start and end apart: 4, of which 2 were waited for; matrix products, arithmetic and copies ran while one was open for 3% of the time, Pallas kernels for 0%

commit v1 on v0

v1 whole, which is shorter than its diff:
```python
import functools

import jax
import jax.numpy as jnp
from jax import lax
from jax.experimental import pallas as pl
from jax.experimental.pallas import tpu as pltpu
from jax.sharding import PartitionSpec as P

F32 = jnp.float32
BF16 = jnp.bfloat16


def halves(x):
    high = x.astype(BF16)
    return high, (x - high.astype(F32)).astype(BF16)


def mix_kernel(half, tap_count, perm_ref, taps_ref, x_ref, lo_ref, hi_ref, s_ref, o_ref,
               x_high, x_low, t_high, t_low, h_ref, y_ref):
    rows = x_ref.shape[0]
    fir = t_high.shape[0]
    window = t_high.shape[1]
    order = h_ref.shape[0]
    groups = rows // order
    per_device = o_ref.shape[1]

    out_id = lax.broadcasted_iota(jnp.int32, (fir, window), 0)
    in_id = lax.broadcasted_iota(jnp.int32, (fir, window), 1)
    lag = in_id - out_id
    band = jnp.zeros((fir, window), F32)
    for k in range(tap_count):
        band = jnp.where(lag == k, taps_ref[k], band)
    t_high[...], t_low[...] = halves(band)
    parity = lax.broadcasted_iota(jnp.int32, (order, order), 0) & lax.broadcasted_iota(
        jnp.int32, (order, order), 1
    )
    for shift in (4, 2, 1):
        parity = parity ^ (parity >> shift)
    h_ref[...] = (1 - 2 * (parity & 1)).astype(F32)

    x_high[0:half, :], x_low[0:half, :] = halves(lo_ref[...])
    x_high[half + rows :, :], x_low[half + rows :, :] = halves(hi_ref[...])

    def split(i, carry):
        at = pl.multiple_of(i * order, order)
        high, low = halves(x_ref[pl.ds(at, order), :])
        to = pl.multiple_of(at + half, half)
        x_high[pl.ds(to, order), :] = high
        x_low[pl.ds(to, order), :] = low
        return carry

    lax.fori_loop(0, groups, split, 0)

    def dot(a, b):
        return jnp.dot(a, b, preferred_element_type=F32)

    def group(a, carry):
        parts = []
        for part in range(order // fir):
            at = pl.multiple_of(a * order + part * fir, fir)
            high = x_high[pl.ds(at, window), :]
            low = x_low[pl.ds(at, window), :]
            parts.append(
                dot(t_high[...], high) + (dot(t_high[...], low) + dot(t_low[...], high))
            )
        filtered = jnp.concatenate(parts, axis=0)
        signed = (h_ref[...] * s_ref[pl.ds(a, 1), :]).astype(BF16)
        high, low = halves(filtered)
        y_ref[a] = dot(signed, high) + dot(signed, low)
        return carry

    lax.fori_loop(0, groups, group, 0)

    tile = 8
    cut = order // per_device

    def butterfly(b, carry):
        at = pl.multiple_of(b * tile, tile)
        values = [y_ref[a, pl.ds(at, tile), :] for a in range(groups)]
        step = 1
        while step < groups:
            for i in range(groups):
                if not i & step:
                    u, v = values[i], values[i + step]
                    values[i], values[i + step] = u + v, u - v
            step *= 2
        part = at // per_device
        row = pl.multiple_of(at % per_device, tile)
        for a in range(groups):
            o_ref[perm_ref[a * cut + part], pl.ds(row, tile), :] = values[a]
        return carry

    lax.fori_loop(0, order // tile, butterfly, 0)


def mixed_chunk(chunk, width, devices, perm, taps, series, low_rows, high_rows, signs):
    rows = series.shape[0]
    half = low_rows.shape[0]
    order = signs.shape[1]
    fir = 128
    spec = lambda r: pl.BlockSpec((r, width), lambda i, *_: (0, chunk))
    slabs = (devices, rows // devices, width)
    return pl.pallas_call(
        functools.partial(mix_kernel, half, taps.shape[0]),
        out_shape=jax.ShapeDtypeStruct(slabs, F32),
        grid_spec=pltpu.PrefetchScalarGridSpec(
            num_scalar_prefetch=2,
            grid=(1,),
            in_specs=[spec(rows), spec(half), spec(half),
                      pl.BlockSpec(signs.shape, lambda i, *_: (0, 0))],
            out_specs=pl.BlockSpec(slabs, lambda i, *_: (0, 0, 0)),
            scratch_shapes=[
                pltpu.VMEM((rows + 2 * half, width), BF16),
                pltpu.VMEM((rows + 2 * half, width), BF16),
                pltpu.VMEM((fir, fir + 2 * half), BF16),
                pltpu.VMEM((fir, fir + 2 * half), BF16),
                pltpu.VMEM((order, order), F32),
                pltpu.VMEM((rows // order, order, width), F32),
            ],
        ),
        cost_estimate=pl.CostEstimate(
            flops=rows * width * 2000, bytes_accessed=rows * width * 8, transcendentals=0
        ),
        name="mix",
    )(perm, taps, series, low_rows, high_rows, signs)


def factor_kernel(block, scale, g_ref, r_ref, m_ref, a_ref):
    size = g_ref.shape[0]
    hi = lax.Precision.HIGHEST
    a_ref[...] = g_ref[...] * scale
    tiles_count = block // 8
    eye_row = lax.broadcasted_iota(jnp.int32, (8, block), 0)
    eye_col = lax.broadcasted_iota(jnp.int32, (8, block), 1)
    sub = lax.broadcasted_iota(jnp.int32, (8, 2 * block), 0)

    def panel(p, carry):
        at = pl.multiple_of(p * block, block)
        tiles = []
        for t in range(tiles_count):
            own = a_ref[pl.ds(pl.multiple_of(at + 8 * t, 8), 8), pl.ds(at, block)]
            unit = (eye_row + 8 * t == eye_col).astype(F32)
            tiles.append(jnp.concatenate([own, unit], axis=1))
        for k in range(block):
            home, row_at = divmod(k, 8)
            row = jnp.broadcast_to(tiles[home][row_at : row_at + 1, :], (8, 2 * block))
            pivot = jnp.broadcast_to(row[:, k : k + 1], (8, 2 * block))
            m_ref[k : k + 1, :] = (row * lax.rsqrt(pivot))[0:1, block:]
            scaled = row / pivot
            for t in range(home, tiles_count):
                column = jnp.broadcast_to(tiles[t][:, k : k + 1], (8, 2 * block))
                if t == home:
                    column = jnp.where(sub > row_at, column, 0.0)
                tiles[t] = tiles[t] - column * scaled
        rows = lax.dot_general(
            m_ref[...], a_ref[pl.ds(at, block), :], (((1,), (0,)), ((), ())),
            precision=hi, preferred_element_type=F32,
        )
        keep = lax.broadcasted_iota(jnp.int32, rows.shape, 1) >= (
            lax.broadcasted_iota(jnp.int32, rows.shape, 0) + at
        )
        rows = jnp.where(keep, rows, 0.0)
        r_ref[pl.ds(at, block), :] = rows

        @pl.when(p < size // block - 1)
        def _():
            a_ref[...] -= lax.dot_general(
                rows, rows, (((0,), (0,)), ((), ())),
                precision=hi, preferred_element_type=F32,
            )
        return carry

    lax.fori_loop(0, size // block, panel, 0)


def factor(gram, sample_count):
    size = gram.shape[0]
    block = min(128, size)
    return pl.pallas_call(
        functools.partial(factor_kernel, block, 1.0 / sample_count),
        out_shape=jax.ShapeDtypeStruct(gram.shape, F32),
        in_specs=[pl.BlockSpec(memory_space=pltpu.VMEM)],
        out_specs=pl.BlockSpec(memory_space=pltpu.VMEM),
        scratch_shapes=[pltpu.VMEM((block, block), F32), pltpu.VMEM((size, size), F32)],
        name="factor",
    )(gram)


def stage_bits(tm, grp):
    grp_bits = list(range(grp.bit_length() - 1))
    base = len(grp_bits)
    tm_bits = list(range(base, base + tm.bit_length() - 1))
    core, rest = tm_bits[:1], tm_bits[1:]
    near, far = rest[: len(rest) // 2], rest[len(rest) // 2 :]
    return core + near + far + grp_bits, core + far + near + grp_bits


def pack(value, bits):
    packed = jnp.zeros_like(value)
    for bit in bits:
        packed = packed * 2 + (value >> bit & 1)
    return packed


def swap_halo(series, half):
    axes = ("tm", "grp")
    count = lax.axis_size(axes)
    forward = [(i, i + 1) for i in range(count - 1)]
    backward = [(i + 1, i) for i in range(count - 1)]
    low = lax.ppermute(series[-half:], axes, forward)
    high = lax.ppermute(series[:half], axes, backward)
    return low, high


def bit_parity(value, bits):
    parity = jnp.zeros_like(value)
    for bit in range(bits):
        parity = parity ^ (value >> bit & 1)
    return parity


CHUNKS = 2


def on_device(series, filter_taps, sign_flips, samples):
    rows_dev, columns = series.shape
    half = (filter_taps.shape[0] - 1) // 2
    tm, grp = lax.axis_size("tm"), lax.axis_size("grp")
    devices = tm * grp
    sample_count = samples.shape[0]
    per_device = rows_dev // devices
    copies = sample_count // rows_dev
    me = lax.axis_index("tm") * grp + lax.axis_index("grp")
    even, odd = stage_bits(tm, grp)
    core = even[0]

    relative = jnp.arange(devices, dtype=jnp.int32) ^ me
    other = relative >> core & 1
    as_even = (me >> core & 1) ^ other == 0
    perm = jnp.where(as_even, pack(relative, even), pack(relative, odd))
    order = min(256, rows_dev)
    signs = sign_flips.astype(F32).reshape(rows_dev // order, order)
    low, high = swap_halo(series, half)

    slot = jnp.arange(devices, dtype=jnp.int32)
    hit = perm[None, :] == slot[:, None]
    owner = (samples // rows_dev).astype(F32).reshape(devices, per_device * copies)
    owner = lax.dot_general(hit.astype(F32), owner, (((1,), (0,)), ((), ())),
                            precision=lax.Precision.HIGHEST).astype(jnp.int32)
    owner = owner[: devices // 2].reshape(devices // 2, per_device, copies).transpose(0, 2, 1)
    low_bit = 1 - (me >> core & 1)
    width = columns // CHUNKS
    tails = []
    for chunk in range(CHUNKS):
        held = mixed_chunk(chunk, width, devices, perm, filter_taps, series, low, high, signs)
        held = held[:, None]
        for even_bit, odd_bit in zip(even, odd):
            count = held.shape[0] // 2
            pairs = []
            for d in range(devices):
                bit = odd_bit if d >> core & 1 else even_bit
                pairs.append((d, d ^ (1 << bit)))
            arrived = lax.ppermute(held[count:], ("tm", "grp"), pairs)
            mine = jnp.where(low_bit == 1, even_bit, odd_bit)
            weight = (1 - 2 * (owner[:count] >> mine & 1)).astype(F32)
            held = held[:count] + weight[..., None] * arrived
        own = owner[0]
        sign = 1 - 2 * bit_parity(own & me, devices.bit_length())
        scale = 1.0 / jnp.sqrt(F32(rows_dev * devices))
        tails.append(held[0] * (sign.astype(F32) * scale)[..., None])
    sketch = jnp.concatenate(tails, axis=-1).transpose(1, 0, 2).reshape(-1, columns)
    local_gram = lax.dot_general(
        sketch, sketch, (((0,), (0,)), ((), ())),
        precision=lax.Precision.HIGHEST, preferred_element_type=F32,
    )
    gram = lax.psum(local_gram, ("tm", "grp"))
    return sketch, factor(gram, sample_count)


def solution(mesh):
    return jax.shard_map(
        on_device,
        mesh=mesh,
        in_specs=(P(("tm", "grp"), None), P(), P(("tm", "grp")), P()),
        out_specs=(P(("tm", "grp"), None), P()),
        check_vma=False,
    )
```

time: 664 us -> 419 us (0.63)
  other arithmetic: 212 us -> 11.3 us
  Pallas kernels: 0 us -> 105 us
  waiting for transfers between devices: 315 us -> 245 us
  matrix products: 47 us -> 2.15 us
  local copies, waits for them, and re-layouts: 54.7 us -> 19.5 us
  starting transfers between devices: 13.3 us -> 22.4 us
    all_to_all x1 -> x0, waiting for transfers between devices: 181 us -> none  [on_device(): lax.all_to_all(outgoing, ('tm', 'grp'), split_axis=0, concat_axis=0, tile...]
    mul x1 -> x2, other arithmetic: 123 us -> 0.17 us  [on_device(): tails.append(held[0] * (sign.astype(F32) * scale)[..., None])]
    ppermute x2 -> x12, waiting for transfers between devices: 0.01 us -> 118 us  [the longest x10 118 us: on_device(): arrived = lax.ppermute(held[count:], ('tm', 'grp'), pairs)]
    pallas_call x0 -> x3, Pallas kernels: none -> 105 us  [the longest x1 75.5 us: factor(): pl.pallas_call(functools.partial(factor_kernel, block, 1.0 / sample_count...]
    another operation x14 -> x0, other arithmetic: 78.8 us -> none  [on_device(): lower = jnp.linalg.cholesky(gram / sample_count)]
    dot_general x3 -> x1, matrix products: 43.1 us -> 0.14 us  [on_device(): lax.dot_general(hit.astype(F32), owner, (((1,), (0,)), ((), ())), precisi...]
    gather x2 -> x0, local copies, waits for them, and re-layouts: 26 us -> none  [the longest x1 21.4 us: on_device(): outgoing = jnp.take(mixed, used_positions, axis=0)]
    ppermute x2 -> x12, starting transfers between devices: 6.24 us -> 22.4 us  [the longest x10 15.5 us: on_device(): arrived = lax.ppermute(held[count:], ('tm', 'grp'), pairs)]
  transfers between devices with their start and end apart: 4 -> 13, of which waited for: 2 -> 10; matrix products, arithmetic and copies ran while one was open for 3% -> 2% of each run, Pallas kernels for 0% -> 3%
where the time goes in v1:
time: 419 us
  waiting for transfers between devices  245 us (58%)
  Pallas kernels  105 us (25%)
  starting transfers between devices  22.4 us (5%)
  local copies, waits for them, and re-layouts  19.5 us (5%)
  between operations  14.3 us (3%)
  other arithmetic  11.3 us (3%)
    psum x1, waiting for transfers between devices, on_device(): gram = lax.psum(local_gram, ('tm', 'grp'))  127 us
    ppermute x10, waiting for transfers between devices, on_device(): arrived = lax.ppermute(held[count:], ('tm', 'grp'), pairs)  118 us
    pallas_call x1, Pallas kernels, factor(): pl.pallas_call(functools.partial(factor_kernel, block, 1.0 / sample_count...  75.5 us
    pallas_call x2, Pallas kernels, mixed_chunk(): pl.pallas_call(functools.partial(mix_kernel, half, taps.shape[0]), out_sh...  29.1 us
    ppermute x10, starting transfers between devices, on_device(): arrived = lax.ppermute(held[count:], ('tm', 'grp'), pairs)  15.5 us
    add x4, other arithmetic, on_device(): held = held[:count] + weight[..., None] * arrived  9.75 us
    slice x2, local copies, waits for them, and re-layouts, on_device(): held = held[:count] + weight[..., None] * arrived  8.64 us
  transfers between devices with their start and end apart: 13, of which 10 were waited for; matrix products, arithmetic and copies ran while one was open for 2% of the time, Pallas kernels for 3%

profile of v1, /device:TPU:0, one launch (start us, length us, event | category | flops | bytes accessed | tf_op | source)
XLA Modules:
  0.0 418.9 jit_solution(4718103934133179084)
XLA Ops:
  9.3 5.6 %collective-permute-start = (f32[16,512]{1,0:T(8,128)S(1)}, f32[16,512]{1,0:T(8,128)S(1)}, u32[]{:S(2)}, u32[]{:S(2)}) collective-permute-start(f32[16,512]{1,0:T(8,128)S(1)} %get-tuple-element.3), channel_id=1, source_target_pairs={{0,1},{1,2},{2,3},{3,4},{4,5},{5,6},{6,7},{7,8},{8,9},{9,10},{10,1... | collective-permute-start | bytes 98312 | tf_op jit(solution)/shard_map/ppermute | solution.py:211
  18.0 14.6 %mix.3 = f32[32,128,256]{2,1,0:T(8,128)} custom-call(s32[32]{0:T(128)} %compare_select_fusion.perm_ref, f32[33]{0:T(128)} %taps_ref.3, f32[4096,512]{1,0:T(8,128)} %x_ref.3, f32[16,512]{1,0:T(8,128)} %copy-done.4, f32[16,512]{1,0:T(8,128)} %copy-done.3, f32[16,256]{1,0:T(8,128)} %reshape.114.s_ref), custom_call_target="tpu_custom_call" | custom-call | flops 2097152000 | bytes 8388608 | tf_op jit(solution)/shard_map/mix/pallas_call | solution.py:104
  32.5 4.0 fusion.28
  36.5 5.1 %collective-permute-start.7 = (f32[16,1,128,256]{3,2,0,1:T(8,128)}, f32[16,1,128,256]{3,2,0,1:T(8,128)}, u32[]{:S(2)}, u32[]{:S(2)}) collective-permute-start(f32[16,1,128,256]{3,2,0,1:T(8,128)} %get-tuple-element.7), channel_id=1, source_target_pairs={{0,4},{1,5},{2,6},{3,7},{4,0},{5,1},{6,2},{7,3},{8,12},{9,13},{10,... | collective-permute-start | bytes 6291464 | tf_op jit(solution)/shard_map/ppermute | solution.py:264
  41.6 14.6 %mix.2 = f32[32,128,256]{2,1,0:T(8,128)} custom-call(s32[32]{0:T(128)} %compare_select_fusion.perm_ref, f32[33]{0:T(128)} %taps_ref.3, f32[4096,512]{1,0:T(8,128)} %x_ref.3, f32[16,512]{1,0:T(8,128)} %copy-done.4, f32[16,512]{1,0:T(8,128)} %copy-done.3, f32[16,256]{1,0:T(8,128)} %reshape.114.s_ref), custom_call_target="tpu_custom_call" | custom-call | flops 2097152000 | bytes 8388608 | tf_op jit(solution)/shard_map/mix/pallas_call | solution.py:104
  56.1 4.7 %fusion.27 = (f32[16,128,256]{2,1,0:T(8,128)}, f32[16,1,128,256]{3,2,0,1:T(8,128)}) fusion(f32[32,128,256]{2,1,0:T(8,128)} %mix.2), kind=kLoop, calls=%fused_computation.56 | loop fusion | bytes 8388608 | tf_op jit(solution)/shard_map/slice | solution.py:267
  61.2 4.1 collective-permute-done.2
  65.3 3.3 multiply_add_fusion.1
  75.4 24.3 %collective-permute-done.8 = f32[8,2,128,256]{3,2,1,0:T(8,128)} collective-permute-done((f32[8,2,128,256]{3,2,1,0:T(8,128)}, f32[8,2,128,256]{3,2,1,0:T(8,128)}, u32[]{:S(2)}, u32[]{:S(2)}) %collective-permute-start.8) | collective-permute-done | bytes 2097184 | tf_op jit(solution)/shard_map/ppermute | solution.py:264
  99.7 22.5 %collective-permute-done.3 = f32[8,2,128,256]{3,2,1,0:T(8,128)} collective-permute-done((f32[8,2,128,256]{3,2,1,0:T(8,128)S(1)}, f32[8,2,128,256]{3,2,1,0:T(8,128)}, u32[]{:S(2)}, u32[]{:S(2)}) %collective-permute-start.3) | collective-permute-done | bytes 2097184 | tf_op jit(solution)/shard_map/ppermute | solution.py:264
  122.2 4.1 slice_add_fusion.1
  128.0 3.3 collective-permute-start.9
  131.4 13.1 %collective-permute-done.9 = f32[4,2,128,256]{3,2,1,0:T(8,128)} collective-permute-done((f32[4,2,128,256]{3,2,1,0:T(8,128)}, f32[4,2,128,256]{3,2,1,0:T(8,128)}, u32[]{:S(2)}, u32[]{:S(2)}) %collective-permute-start.9) | collective-permute-done | bytes 1048608 | tf_op jit(solution)/shard_map/ppermute | solution.py:264
  144.4 11.2 %collective-permute-done.4 = f32[4,2,128,256]{3,2,1,0:T(8,128)} collective-permute-done((f32[4,2,128,256]{3,2,1,0:T(8,128)S(1)}, f32[4,2,128,256]{3,2,1,0:T(8,128)}, u32[]{:S(2)}, u32[]{:S(2)}) %collective-permute-start.4) | collective-permute-done | bytes 1048608 | tf_op jit(solution)/shard_map/ppermute | solution.py:264
  155.7 2.1 slice_add_fusion.3
  158.0 2.0 collective-permute-start.5
  160.0 12.8 %collective-permute-done.10 = f32[2,2,128,256]{3,2,1,0:T(8,128)S(1)} collective-permute-done((f32[2,2,128,256]{3,2,1,0:T(8,128)S(1)}, f32[2,2,128,256]{3,2,1,0:T(8,128)S(1)}, u32[]{:S(2)}, u32[]{:S(2)}) %collective-permute-start.10) | collective-permute-done | bytes 524320 | tf_op jit(solution)/shard_map/ppermute | solution.py:264
  172.7 8.9 %collective-permute-done.5 = f32[2,2,128,256]{3,2,1,0:T(8,128)S(1)} collective-permute-done((f32[2,2,128,256]{3,2,1,0:T(8,128)S(1)}, f32[2,2,128,256]{3,2,1,0:T(8,128)S(1)}, u32[]{:S(2)}, u32[]{:S(2)}) %collective-permute-start.5) | collective-permute-done | bytes 524320 | tf_op jit(solution)/shard_map/ppermute | solution.py:264
  182.0 2.9 collective-permute-start.6
  184.9 15.3 %collective-permute-done.11 = f32[1,2,128,256]{3,2,1,0:T(8,128)S(1)} collective-permute-done((f32[1,2,128,256]{3,2,1,0:T(8,128)S(1)}, f32[1,2,128,256]{3,2,1,0:T(8,128)S(1)}, u32[]{:S(2)}, u32[]{:S(2)}) %collective-permute-start.11) | collective-permute-done | bytes 262176 | tf_op jit(solution)/shard_map/ppermute | solution.py:264
  200.2 5.5 %collective-permute-done.6 = f32[1,2,128,256]{3,2,1,0:T(8,128)S(1)} collective-permute-done((f32[1,2,128,256]{3,2,1,0:T(8,128)S(1)}, f32[1,2,128,256]{3,2,1,0:T(8,128)S(1)}, u32[]{:S(2)}, u32[]{:S(2)}) %collective-permute-start.6) | collective-permute-done | bytes 262176 | tf_op jit(solution)/shard_map/ppermute | solution.py:264
  205.9 2.0 convolution_bitcast_fusion
  209.6 127.0 %all-reduce.2.cloned.1.call-done.g_ref = f32[512,512]{1,0:T(8,128)} async-done(((f32[512,512]{1,0:T(8,128)}), f32[512,512]{1,0:T(8,128)}) %all-reduce.2.cloned.1.call-update) | async-done | bytes 1048592 | tf_op jit(solution)/shard_map/psum | solution.py:277
  336.6 75.5 %factor.1 = f32[512,512]{1,0:T(8,128)} custom-call(f32[512,512]{1,0:T(8,128)} %all-reduce.2.cloned.1.call-done.g_ref), custom_call_target="tpu_custom_call" | custom-call | tf_op jit(solution)/shard_map/factor/pallas_call | solution.py:180
  (60 shorter events, 16.3 us)
Async XLA Ops:
  7.2 329.4 %all-reduce.2.cloned.1.call-start = ((), (), s32[]{:S(2)}) async-start(), calls=%async_computation | async-start | bytes 2097152 | tf_op jit(solution)/shard_map/psum | solution.py:277
  8.0 8.7 %collective-permute-start.1 = (f32[16,512]{1,0:T(8,128)S(1)}, f32[16,512]{1,0:T(8,128)S(1)}, u32[]{:S(2)}, u32[]{:S(2)}) collective-permute-start(f32[16,512]{1,0:T(8,128)S(1)} %get-tuple-element.2), channel_id=1, source_target_pairs={{1,0},{2,1},{3,2},{4,3},{5,4},{6,5},{7,6},{8,7},{9,8},{10,9},{11,1... | collective-permute-start | bytes 98312 | tf_op jit(solution)/shard_map/ppermute | solution.py:212
  9.3 7.5 %collective-permute-start = (f32[16,512]{1,0:T(8,128)S(1)}, f32[16,512]{1,0:T(8,128)S(1)}, u32[]{:S(2)}, u32[]{:S(2)}) collective-permute-start(f32[16,512]{1,0:T(8,128)S(1)} %get-tuple-element.3), channel_id=1, source_target_pairs={{0,1},{1,2},{2,3},{3,4},{4,5},{5,6},{6,7},{7,8},{8,9},{9,10},{10,1... | collective-permute-start | bytes 98312 | tf_op jit(solution)/shard_map/ppermute | solution.py:211
  16.7 0.6 copy-start.3
  17.4 0.6 copy-start.4
  36.5 24.7 %collective-permute-start.7 = (f32[16,1,128,256]{3,2,0,1:T(8,128)}, f32[16,1,128,256]{3,2,0,1:T(8,128)}, u32[]{:S(2)}, u32[]{:S(2)}) collective-permute-start(f32[16,1,128,256]{3,2,0,1:T(8,128)} %get-tuple-element.7), channel_id=1, source_target_pairs={{0,4},{1,5},{2,6},{3,7},{4,0},{5,1},{6,2},{7,3},{8,12},{9,13},{10,... | collective-permute-start | bytes 6291464 | tf_op jit(solution)/shard_map/ppermute | solution.py:264
  56.1 4.7 %copy-start.5 = (s32[8192]{0:T(1024)S(1)}, s32[8192]{0:T(1024)}, u32[]{:S(2)}) copy-start(s32[8192]{0:T(1024)} %param.7) | copy-start | bytes 98308
  56.1 4.7 %copy-start.6 = (s32[32]{0:T(128)S(1)}, s32[32]{0:T(128)}, u32[]{:S(2)}) copy-start(s32[32]{0:T(128)} %compare_select_fusion.perm_ref) | copy-start | bytes 388
  60.8 4.5 %collective-permute-start.2 = (f32[16,1,128,256]{3,2,0,1:T(8,128)}, f32[16,1,128,256]{3,2,0,1:T(8,128)}, u32[]{:S(2)}, u32[]{:S(2)}) collective-permute-start(f32[16,1,128,256]{3,2,0,1:T(8,128)} %get-tuple-element.5), channel_id=1, source_target_pairs={{0,4},{1,5},{2,6},{3,7},{4,0},{5,1},{6,2},{7,3},{8,12},{9,13},{10,... | collective-permute-start | bytes 6291464 | tf_op jit(solution)/shard_map/ppermute | solution.py:264
  68.6 2.0 copy-start
  68.6 3.3 copy-start.1
  73.4 26.4 %collective-permute-start.8 = (f32[8,2,128,256]{3,2,1,0:T(8,128)}, f32[8,2,128,256]{3,2,1,0:T(8,128)}, u32[]{:S(2)}, u32[]{:S(2)}) collective-permute-start(f32[8,2,128,256]{3,2,1,0:T(8,128)} %slice.142), channel_id=1, source_target_pairs={{0,8},{1,9},{2,10},{3,11},{4,20},{5,21},{6,22},{7,23},{8,0},{9,1},... | collective-permute-start | bytes 6291464 | tf_op jit(solution)/shard_map/ppermute | solution.py:264
  75.2 47.0 %collective-permute-start.3 = (f32[8,2,128,256]{3,2,1,0:T(8,128)S(1)}, f32[8,2,128,256]{3,2,1,0:T(8,128)}, u32[]{:S(2)}, u32[]{:S(2)}) collective-permute-start(f32[8,2,128,256]{3,2,1,0:T(8,128)S(1)} %slice.129), channel_id=1, source_target_pairs={{0,8},{1,9},{2,10},{3,11},{4,20},{5,21},{6,22},{7,23},{8,0},{9,1},... | collective-permute-start | bytes 6291464 | tf_op jit(solution)/shard_map/ppermute | solution.py:264
  126.3 1.7 copy-start.2
  128.0 16.4 %collective-permute-start.9 = (f32[4,2,128,256]{3,2,1,0:T(8,128)}, f32[4,2,128,256]{3,2,1,0:T(8,128)}, u32[]{:S(2)}, u32[]{:S(2)}) collective-permute-start(f32[4,2,128,256]{3,2,1,0:T(8,128)} %slice.144), channel_id=1, source_target_pairs={{0,16},{1,17},{2,18},{3,19},{4,12},{5,13},{6,14},{7,15},{8,24},{9,... | collective-permute-start | bytes 3145736 | tf_op jit(solution)/shard_map/ppermute | solution.py:264
  131.3 24.3 %collective-permute-start.4 = (f32[4,2,128,256]{3,2,1,0:T(8,128)S(1)}, f32[4,2,128,256]{3,2,1,0:T(8,128)}, u32[]{:S(2)}, u32[]{:S(2)}) collective-permute-start(f32[4,2,128,256]{3,2,1,0:T(8,128)S(1)} %slice.132), channel_id=1, source_target_pairs={{0,16},{1,17},{2,18},{3,19},{4,12},{5,13},{6,14},{7,15},{8,24},{9,... | collective-permute-start | bytes 3145736 | tf_op jit(solution)/shard_map/ppermute | solution.py:264
  157.9 14.9 %collective-permute-start.10 = (f32[2,2,128,256]{3,2,1,0:T(8,128)S(1)}, f32[2,2,128,256]{3,2,1,0:T(8,128)S(1)}, u32[]{:S(2)}, u32[]{:S(2)}) collective-permute-start(f32[2,2,128,256]{3,2,1,0:T(8,128)S(1)} %slice.146), channel_id=1, source_target_pairs={{0,1},{1,0},{2,3},{3,2},{4,5},{5,4},{6,7},{7,6},{8,9},{9,8},{10,11... | collective-permute-start | bytes 1572872 | tf_op jit(solution)/shard_map/ppermute | solution.py:264
  158.0 23.7 %collective-permute-start.5 = (f32[2,2,128,256]{3,2,1,0:T(8,128)S(1)}, f32[2,2,128,256]{3,2,1,0:T(8,128)S(1)}, u32[]{:S(2)}, u32[]{:S(2)}) collective-permute-start(f32[2,2,128,256]{3,2,1,0:T(8,128)S(1)} %slice.135), channel_id=1, source_target_pairs={{0,1},{1,0},{2,3},{3,2},{4,5},{5,4},{6,7},{7,6},{8,9},{9,8},{10,11... | collective-permute-start | bytes 1572872 | tf_op jit(solution)/shard_map/ppermute | solution.py:264
  181.9 18.3 %collective-permute-start.11 = (f32[1,2,128,256]{3,2,1,0:T(8,128)S(1)}, f32[1,2,128,256]{3,2,1,0:T(8,128)S(1)}, u32[]{:S(2)}, u32[]{:S(2)}) collective-permute-start(f32[1,2,128,256]{3,2,1,0:T(8,128)S(1)} %slice.148), channel_id=1, source_target_pairs={{0,2},{1,3},{2,0},{3,1},{4,6},{5,7},{6,4},{7,5},{8,10},{9,11},{10,... | collective-permute-start | bytes 786440 | tf_op jit(solution)/shard_map/ppermute | solution.py:264
  182.0 23.7 %collective-permute-start.6 = (f32[1,2,128,256]{3,2,1,0:T(8,128)S(1)}, f32[1,2,128,256]{3,2,1,0:T(8,128)S(1)}, u32[]{:S(2)}, u32[]{:S(2)}) collective-permute-start(f32[1,2,128,256]{3,2,1,0:T(8,128)S(1)} %slice.138), channel_id=1, source_target_pairs={{0,2},{1,3},{2,0},{3,1},{4,6},{5,7},{6,4},{7,5},{8,10},{9,11},{10,... | collective-permute-start | bytes 786440 | tf_op jit(solution)/shard_map/ppermute | solution.py:264
Sparse Core Ops, SparseCore 0:
  208.1 128.4 all-reduce.1

commit v2 on v1

--- a/solution.py
+++ b/solution.py
@@ -94,22 +94,23 @@
     lax.fori_loop(0, order // tile, butterfly, 0)
 
 
-def mixed_chunk(chunk, width, devices, perm, taps, series, low_rows, high_rows, signs):
-    rows = series.shape[0]
+def mixed(devices, perm, taps, series, low_rows, high_rows, signs):
+    rows, columns = series.shape
     half = low_rows.shape[0]
     order = signs.shape[1]
     fir = 128
-    spec = lambda r: pl.BlockSpec((r, width), lambda i, *_: (0, chunk))
-    slabs = (devices, rows // devices, width)
+    width = columns // CHUNKS
+    spec = lambda r: pl.BlockSpec((r, width), lambda i, *_: (0, i))
+    per_device = rows // devices
     return pl.pallas_call(
         functools.partial(mix_kernel, half, taps.shape[0]),
-        out_shape=jax.ShapeDtypeStruct(slabs, F32),
+        out_shape=jax.ShapeDtypeStruct((devices, per_device, columns), F32),
         grid_spec=pltpu.PrefetchScalarGridSpec(
             num_scalar_prefetch=2,
-            grid=(1,),
+            grid=(CHUNKS,),
             in_specs=[spec(rows), spec(half), spec(half),
                       pl.BlockSpec(signs.shape, lambda i, *_: (0, 0))],
-            out_specs=pl.BlockSpec(slabs, lambda i, *_: (0, 0, 0)),
+            out_specs=pl.BlockSpec((devices, per_device, width), lambda i, *_: (0, 0, i)),
             scratch_shapes=[
                 pltpu.VMEM((rows + 2 * half, width), BF16),
                 pltpu.VMEM((rows + 2 * half, width), BF16),
@@ -119,40 +120,68 @@
                 pltpu.VMEM((rows // order, order, width), F32),
             ],
         ),
-        cost_estimate=pl.CostEstimate(
-            flops=rows * width * 2000, bytes_accessed=rows * width * 8, transcendentals=0
-        ),
         name="mix",
     )(perm, taps, series, low_rows, high_rows, signs)
 
 
 def factor_kernel(block, scale, g_ref, r_ref, m_ref, a_ref):
-    size = g_ref.shape[0]
+    size = a_ref.shape[0]
     hi = lax.Precision.HIGHEST
-    a_ref[...] = g_ref[...] * scale
+    a_ref[...] = jnp.zeros_like(a_ref)
+    for q, (i, j) in enumerate(upper_blocks(size // block)):
+        depth = block // 8
+        part = g_ref[q * depth : (q + 1) * depth].reshape(block, block)
+        a_ref[i * block : (i + 1) * block, j * block : (j + 1) * block] = part * scale
     tiles_count = block // 8
     eye_row = lax.broadcasted_iota(jnp.int32, (8, block), 0)
     eye_col = lax.broadcasted_iota(jnp.int32, (8, block), 1)
-    sub = lax.broadcasted_iota(jnp.int32, (8, 2 * block), 0)
+    step = 4
+
+    def lane(value, k):
+        return jnp.broadcast_to(value[:, k : k + 1], (8, block))
 
     def panel(p, carry):
         at = pl.multiple_of(p * block, block)
-        tiles = []
+        left, right = [], []
         for t in range(tiles_count):
-            own = a_ref[pl.ds(pl.multiple_of(at + 8 * t, 8), 8), pl.ds(at, block)]
-            unit = (eye_row + 8 * t == eye_col).astype(F32)
-            tiles.append(jnp.concatenate([own, unit], axis=1))
-        for k in range(block):
-            home, row_at = divmod(k, 8)
-            row = jnp.broadcast_to(tiles[home][row_at : row_at + 1, :], (8, 2 * block))
-            pivot = jnp.broadcast_to(row[:, k : k + 1], (8, 2 * block))
-            m_ref[k : k + 1, :] = (row * lax.rsqrt(pivot))[0:1, block:]
-            scaled = row / pivot
-            for t in range(home, tiles_count):
-                column = jnp.broadcast_to(tiles[t][:, k : k + 1], (8, 2 * block))
-                if t == home:
-                    column = jnp.where(sub > row_at, column, 0.0)
-                tiles[t] = tiles[t] - column * scaled
+            left.append(a_ref[pl.ds(pl.multiple_of(at + 8 * t, 8), 8), pl.ds(at, block)])
+            right.append((eye_row + 8 * t == eye_col).astype(F32))
+        for k in range(0, block, step):
+            home, top = divmod(k, 8)
+            spread = lambda v, r: jnp.broadcast_to(v[r : r + 1, :], (8, block))
+            rows_l = [spread(left[home], top + j) for j in range(step)]
+            rows_r = [spread(right[home], top + j) for j in range(step)]
+            corner = {(i, j): lane(rows_l[i], k + j) for i in range(step) for j in range(i, step)}
+            inverse, link = [], {}
+            for j in range(step):
+                inverse.append(lax.rsqrt(corner[j, j]))
+                for i in range(j + 1, step):
+                    link[j, i] = corner[j, i] * inverse[j]
+                for i in range(j + 1, step):
+                    for h in range(i, step):
+                        corner[i, h] = corner[i, h] - link[j, i] * link[j, h]
+
+            def solve(values):
+                done = []
+                for j in range(step):
+                    value = values[j]
+                    for i in range(j):
+                        value = value - link[i, j] * done[i]
+                    done.append(value * inverse[j])
+                return done
+
+            rows_l, rows_r = solve(rows_l), solve(rows_r)
+            for j in range(step):
+                m_ref[k + j : k + j + 1, :] = rows_r[j][0:1, :]
+            first = home if top + step < 8 else home + 1
+            for t in range(first, tiles_count):
+                columns = solve([lane(left[t], k + j) for j in range(step)])
+                for j in range(step):
+                    column = columns[j]
+                    if t == home:
+                        column = jnp.where(eye_row >= top + step, column, 0.0)
+                    left[t] = left[t] - column * rows_l[j]
+                    right[t] = right[t] - column * rows_r[j]
         rows = lax.dot_general(
             m_ref[...], a_ref[pl.ds(at, block), :], (((1,), (0,)), ((), ())),
             precision=hi, preferred_element_type=F32,
@@ -174,17 +203,185 @@
     lax.fori_loop(0, size // block, panel, 0)
 
 
-def factor(gram, sample_count):
-    size = gram.shape[0]
-    block = min(128, size)
+BLOCK = 128
+
+
+def upper_blocks(count):
+    return [(i, j) for i in range(count) for j in range(i, count)]
+
+
+def factor(packed, size, sample_count):
     return pl.pallas_call(
-        functools.partial(factor_kernel, block, 1.0 / sample_count),
-        out_shape=jax.ShapeDtypeStruct(gram.shape, F32),
+        functools.partial(factor_kernel, BLOCK, 1.0 / sample_count),
+        out_shape=jax.ShapeDtypeStruct((size, size), F32),
         in_specs=[pl.BlockSpec(memory_space=pltpu.VMEM)],
         out_specs=pl.BlockSpec(memory_space=pltpu.VMEM),
-        scratch_shapes=[pltpu.VMEM((block, block), F32), pltpu.VMEM((size, size), F32)],
+        scratch_shapes=[pltpu.VMEM((BLOCK, BLOCK), F32), pltpu.VMEM((size, size), F32)],
         name="factor",
-    )(gram)
+    )(packed)
+
+
+PIECES = 4
+
+
+def exchange_kernel(tm, grp, scale, held_ref, owner_ref, sk_ref, gram_ref, *scratch):
+    tm_bits, grp_bits = tm.bit_length() - 1, grp.bit_length() - 1
+    stages = tm_bits + grp_bits
+    kept, sums, part = scratch[0], scratch[1], scratch[2]
+    arrived = scratch[3 : 3 + stages]
+    landed = scratch[3 + stages : 3 + 2 * stages]
+    keep_sem, send_sem, recv_sem = scratch[3 + 2 * stages :]
+    t, g = lax.axis_index("tm"), lax.axis_index("grp")
+    core = t % 2
+    devices = tm * grp
+    pieces, width = kept.shape[0], kept.shape[3]
+    depth = kept.shape[2]
+
+    def across_tm(bit):
+        value = (t // 2**bit) % 2
+        return value, (t + (1 - 2 * value) * 2**bit, g)
+
+    peers = [across_tm(0)]
+    rest = list(range(1, tm_bits))
+    near, far = rest[: len(rest) // 2], rest[len(rest) // 2 :]
+    for even, odd in zip(near + far, far + near):
+        (v0, p0), (v1, p1) = across_tm(even), across_tm(odd)
+        mix = lambda u, v: u * (1 - core) + v * core
+        peers.append((mix(v0, v1), (mix(p0[0], p1[0]), g)))
+    for bit in range(grp_bits):
+        value = (g // 2**bit) % 2
+        peers.append((value, (t, g + (1 - 2 * value) * 2**bit)))
+
+    barrier = pltpu.get_barrier_semaphore()
+    for value, peer in peers:
+        pl.semaphore_signal(barrier, inc=1, device_id=peer, device_id_type=pl.DeviceIdType.MESH)
+    pl.semaphore_wait(barrier, stages)
+
+    def remote(source, target, slot, stage):
+        return pltpu.make_async_remote_copy(
+            src_ref=source, dst_ref=target, send_sem=send_sem.at[slot],
+            recv_sem=recv_sem.at[slot], device_id=peers[stage][1],
+            device_id_type=pl.DeviceIdType.MESH,
+        )
+
+    copies, keeps = {}, []
+    for c in range(pieces):
+        span = pl.ds(c * depth, depth)
+        copies[c, 0] = remote(held_ref.at[pl.ds(devices // 2, devices // 2), span, :],
+                              arrived[0].at[c], c, 0)
+        copies[c, 0].start()
+        keeps.append(pltpu.make_async_copy(
+            held_ref.at[pl.ds(0, devices // 2), span, :], kept.at[c], keep_sem.at[c]))
+        keeps[c].start()
+
+    def weight(c, s, k, bit):
+        code = owner_ref[s, k, pl.ds(c * depth, depth), :]
+        sign = (1 - 2 * ((code >> bit) & 1)).astype(F32)
+        return jnp.concatenate([sign] * (width // code.shape[1]), axis=1)
+
+    def combine(c, stage, count):
+        def slab(s, carry):
+            for k in range(2):
+                value = weight(c, s, k, stage)
+                if stage == 0:
+                    sums[c, s, k] = kept[c, s] + value * arrived[0][c, s]
+                else:
+                    sums[c, s, k] = sums[c, s, k] + value * arrived[stage][c, s, k]
+            return carry
+
+        lax.fori_loop(0, count, slab, 0)
+
+    order = sorted(
+        ((c, i) for c in range(pieces) for i in range(stages)),
+        key=lambda ci: (0 if ci[1] == 0 else 2 * ci[0] + ci[1], ci[1], ci[0]),
+    )
+    for c, i in order:
+        if i == 0:
+            keeps[c].wait()
+        copies[c, i].wait_recv()
+        count = devices >> (i + 1)
+        combine(c, i, count)
+        if i + 1 < stages:
+            after = count // 2
+            copies[c, i + 1] = remote(
+                sums.at[c, pl.ds(after, after)], arrived[i + 1].at[c],
+                (i + 1) * pieces + c, i + 1)
+            copies[c, i + 1].start()
+        else:
+            for k in range(2):
+                sk_ref[k, pl.ds(c * depth, depth), :] = (
+                    sums[c, 0, k] * (weight(c, 0, k, stages) * scale))
+
+    blocks = width // BLOCK
+    rows = BLOCK // 8
+    total = part.shape[0]
+    sketch = sk_ref[...].reshape(2 * pieces * depth, width)
+    q = 0
+    for i in range(blocks):
+        product = lax.dot_general(
+            sketch[:, i * BLOCK : (i + 1) * BLOCK], sketch[:, i * BLOCK :],
+            (((0,), (0,)), ((), ())),
+            precision=lax.Precision.HIGHEST, preferred_element_type=F32)
+        for j in range(blocks - i):
+            part[q * rows : (q + 1) * rows] = product[:, j * BLOCK : (j + 1) * BLOCK].reshape(
+                rows, 8, BLOCK)
+            q += 1
+    if q * rows < total:
+        part[q * rows :] = jnp.zeros((total - q * rows, 8, BLOCK), F32)
+    offset, size = 0, total
+    base = stages * pieces
+    for i in range(stages):
+        size //= 2
+        value = peers[i][0]
+        copies[i] = remote(part.at[pl.ds(offset + (1 - value) * size, size)],
+                           landed[i], base + i, i)
+        copies[i].start()
+        offset = offset + value * size
+        copies[i].wait_recv()
+        part[pl.ds(offset, size)] = part[pl.ds(offset, size)] + landed[i][...]
+    gram_ref[pl.ds(offset, size)] = part[pl.ds(offset, size)]
+    for i in reversed(range(stages)):
+        slot = base + stages + i
+        span = pl.ds(offset, size)
+        back = remote(gram_ref.at[span], gram_ref.at[span], slot, i)
+        back.start()
+        back.wait()
+        offset = offset - peers[i][0] * size
+        size *= 2
+    for copy in copies.values():
+        copy.wait_send()
+
+
+def exchange(tm, grp, scale, held, owners):
+    devices, per_device, width = held.shape
+    stages = (tm * grp).bit_length() - 1
+    pieces = min(PIECES, per_device // 8)
+    depth = per_device // pieces
+    blocks = width // BLOCK
+    needed = blocks * (blocks + 1) // 2 * (BLOCK // 8)
+    total = -(-needed // devices) * devices
+    sem = pltpu.SemaphoreType.DMA
+    arrived = [pltpu.VMEM((pieces, devices // 2, depth, width), F32)] + [
+        pltpu.VMEM((pieces, devices >> (i + 1), 2, depth, width), F32) for i in range(1, stages)]
+    landed = [pltpu.VMEM((total >> (i + 1), 8, BLOCK), F32) for i in range(stages)]
+    return pl.pallas_call(
+        functools.partial(exchange_kernel, tm, grp, scale),
+        out_shape=(jax.ShapeDtypeStruct((2, per_device, width), F32),
+                   jax.ShapeDtypeStruct((total, 8, BLOCK), F32)),
+        in_specs=[pl.BlockSpec(memory_space=pl.ANY), pl.BlockSpec(memory_space=pltpu.VMEM)],
+        out_specs=(pl.BlockSpec(memory_space=pltpu.VMEM),) * 2,
+        scratch_shapes=[
+            pltpu.VMEM((pieces, devices // 2, depth, width), F32),
+            pltpu.VMEM((pieces, devices // 2, 2, depth, width), F32),
+            pltpu.VMEM((total, 8, BLOCK), F32),
+            *arrived, *landed,
+            sem((pieces,)), sem((stages * pieces + 2 * stages,)),
+            sem((stages * pieces + 2 * stages,)),
+        ],
+        compiler_params=pltpu.CompilerParams(
+            collective_id=0, has_side_effects=True, vmem_limit_bytes=60 * 2**20),
+        name="exchange",
+    )(held, owners)
 
 
 def stage_bits(tm, grp):
@@ -249,33 +446,17 @@
     owner = lax.dot_general(hit.astype(F32), owner, (((1,), (0,)), ((), ())),
                             precision=lax.Precision.HIGHEST).astype(jnp.int32)
     owner = owner[: devices // 2].reshape(devices // 2, per_device, copies).transpose(0, 2, 1)
-    low_bit = 1 - (me >> core & 1)
-    width = columns // CHUNKS
-    tails = []
-    for chunk in range(CHUNKS):
-        held = mixed_chunk(chunk, width, devices, perm, filter_taps, series, low, high, signs)
-        held = held[:, None]
-        for even_bit, odd_bit in zip(even, odd):
-            count = held.shape[0] // 2
-            pairs = []
-            for d in range(devices):
-                bit = odd_bit if d >> core & 1 else even_bit
-                pairs.append((d, d ^ (1 << bit)))
-            arrived = lax.ppermute(held[count:], ("tm", "grp"), pairs)
-            mine = jnp.where(low_bit == 1, even_bit, odd_bit)
-            weight = (1 - 2 * (owner[:count] >> mine & 1)).astype(F32)
-            held = held[:count] + weight[..., None] * arrived
-        own = owner[0]
-        sign = 1 - 2 * bit_parity(own & me, devices.bit_length())
-        scale = 1.0 / jnp.sqrt(F32(rows_dev * devices))
-        tails.append(held[0] * (sign.astype(F32) * scale)[..., None])
-    sketch = jnp.concatenate(tails, axis=-1).transpose(1, 0, 2).reshape(-1, columns)
-    local_gram = lax.dot_general(
-        sketch, sketch, (((0,), (0,)), ((), ())),
-        precision=lax.Precision.HIGHEST, preferred_element_type=F32,
-    )
-    gram = lax.psum(local_gram, ("tm", "grp"))
-    return sketch, factor(gram, sample_count)
+    is_even = (me >> core & 1) == 0
+    code = jnp.zeros_like(owner)
+    for stage, (even_bit, odd_bit) in enumerate(zip(even, odd)):
+        code = code + ((owner >> jnp.where(is_even, even_bit, odd_bit) & 1) << stage)
+    code = code + (bit_parity(owner & me, devices.bit_length()) << len(even))
+    codes = jnp.broadcast_to(code[..., None], code.shape + (BLOCK,))
+    held = mixed(devices, perm, filter_taps, series, low, high, signs)
+    scale = (rows_dev * devices) ** -0.5
+    sums, packed = exchange(tm, grp, scale, held, codes)
+    sketch = sums.transpose(1, 0, 2).reshape(-1, columns)
+    return sketch, factor(packed, columns, sample_count)
 
 
 def solution(mesh):

time: 419 us -> 202 us (0.48)
  waiting for transfers between devices: 245 us -> 0.01 us
  Pallas kernels: 105 us -> 185 us
  starting transfers between devices: 22.4 us -> 6.87 us
  between operations: 14.3 us -> 0.74 us
  local copies, waits for them, and re-layouts: 19.5 us -> 7.08 us
  other arithmetic: 11.3 us -> 1.56 us
    psum x1 -> x0, waiting for transfers between devices: 127 us -> none  [on_device(): gram = lax.psum(local_gram, ('tm', 'grp'))]
    ppermute x10 -> x0, waiting for transfers between devices: 118 us -> none  [on_device(): arrived = lax.ppermute(held[count:], ('tm', 'grp'), pairs)]
    pallas_call x3, Pallas kernels: 105 us -> 185 us  [the longest x1 131 us: exchange(): pl.pallas_call(functools.partial(exchange_kernel, tm, grp, scale), out_sh...]
    ppermute x10 -> x0, starting transfers between devices: 15.5 us -> none  [on_device(): arrived = lax.ppermute(held[count:], ('tm', 'grp'), pairs)]
    slice x11 -> x0, local copies, waits for them, and re-layouts: 11.6 us -> none  [the longest x2 8.64 us: on_device(): held = held[:count] + weight[..., None] * arrived]
    add x4 -> x1, other arithmetic: 9.75 us -> 0.03 us  [on_device(): code = code + (bit_parity(owner & me, devices.bit_length()) << len(even))]
  transfers between devices with their start and end apart: 13 -> 2, of which waited for: 10 -> 0; matrix products, arithmetic and copies ran while one was open for 2% -> 1% of each run, Pallas kernels for 3% -> 0%
where the time goes in v2:
time: 202 us; the launch traced here: 201 us
  Pallas kernels  185 us (92%)
  local copies, waits for them, and re-layouts  7.08 us (4%)
  starting transfers between devices  6.87 us (3%)
    pallas_call x1, Pallas kernels, exchange(): pl.pallas_call(functools.partial(exchange_kernel, tm, grp, scale), out_sh...  131 us
    pallas_call x1, Pallas kernels, factor(): pl.pallas_call(functools.partial(factor_kernel, BLOCK, 1.0 / sample_count...  28.8 us
    pallas_call x1, Pallas kernels, mixed(): pl.pallas_call(functools.partial(mix_kernel, half, taps.shape[0]), out_sh...  25.5 us
    ppermute x1, starting transfers between devices, swap_halo(): low = lax.ppermute(series[-half:], axes, forward)  5.59 us
  transfers between devices with their start and end apart: 2, of which 0 were waited for; matrix products, arithmetic and copies ran while one was open for 1% of the time, Pallas kernels for 0%

profile of v2, /device:TPU:0, one launch (start us, length us, event | category | flops | bytes accessed | tf_op | source)
XLA Modules:
  0.0 201.5 jit_solution(17623501557346485527)
XLA Ops:
  0.6 0.8 fusion.5
  1.4 1.3 collective-permute-start.1
  2.7 5.6 %collective-permute-start = (f32[16,512]{1,0:T(8,128)S(1)}, f32[16,512]{1,0:T(8,128)S(1)}, u32[]{:S(2)}, u32[]{:S(2)}) collective-permute-start(f32[16,512]{1,0:T(8,128)S(1)} %get-tuple-element.7), channel_id=1, source_target_pairs={{0,1},{1,2},{2,3},{3,4},{4,5},{5,6},{6,7},{7,8},{8,9},{9,10},{10,1... | collective-permute-start | bytes 98312 | tf_op jit(solution)/shard_map/ppermute | solution.py:408
  8.3 0.0 copy-start.2
  8.3 0.8 fusion.1
  9.1 0.1 fusion.3
  9.3 0.7 convert_element_type.10
  10.0 0.6 reshape.103.s_ref
  10.7 0.1 copy.7
  10.8 0.1 copy.8
  10.8 0.0 collective-permute-done.1.hi_ref
  10.8 0.0 copy-start
  10.8 0.0 collective-permute-done.lo_ref
  10.9 0.0 copy-done.2
  10.9 0.6 copy-done
  11.5 0.0 copy-start.1
  11.5 0.6 copy-done.1
  12.1 25.5 %mix.1.held_ref = f32[32,128,512]{2,1,0:T(8,128)} custom-call(s32[32]{0:T(128)} %copy-done.2, f32[33]{0:T(128)} %taps_ref.1, f32[4096,512]{1,0:T(8,128)} %x_ref.1, f32[16,512]{1,0:T(8,128)} %copy-done.1, f32[16,512]{1,0:T(8,128)} %copy-done, f32[16,256]{1,0:T(8,128)} %reshape.103.s_ref), custom_call_target="tpu_custom_call" | custom-call | tf_op jit(solution)/shard_map/mix/pallas_call | solution.py:105
  37.6 1.7 broadcast_in_dim.2.owner_ref
  39.3 130.7 %exchange.1 = (f32[2,128,512]{2,1,0:T(8,128)}, f32[160,8,128]{2,1,0:T(8,128)}) custom-call(f32[32,128,512]{2,1,0:T(8,128)} %mix.1.held_ref, s32[16,2,128,128]{3,2,1,0:T(8,128)} %broadcast_in_dim.2.owner_ref), custom_call_target="tpu_custom_call" | custom-call | tf_op jit(solution)/shard_map/exchange/pallas_call | solution.py:367
  170.1 1.4 copy.9
  171.5 1.2 reshape.105
  172.7 28.8 %factor.1 = f32[512,512]{1,0:T(8,128)} custom-call(f32[160,8,128]{2,1,0:T(8,128)} %get-tuple-element.5.g_ref), custom_call_target="tpu_custom_call" | custom-call | tf_op jit(solution)/shard_map/factor/pallas_call | solution.py:214
  (3 shorter events, 0.1 us)
Async XLA Ops:
  1.4 9.4 %collective-permute-start.1 = (f32[16,512]{1,0:T(8,128)S(1)}, f32[16,512]{1,0:T(8,128)S(1)}, u32[]{:S(2)}, u32[]{:S(2)}) collective-permute-start(f32[16,512]{1,0:T(8,128)S(1)} %get-tuple-element.6), channel_id=1, source_target_pairs={{1,0},{2,1},{3,2},{4,3},{5,4},{6,5},{7,6},{8,7},{9,8},{10,9},{11,1... | collective-permute-start | bytes 98312 | tf_op jit(solution)/shard_map/ppermute | solution.py:409
  2.7 8.1 %collective-permute-start = (f32[16,512]{1,0:T(8,128)S(1)}, f32[16,512]{1,0:T(8,128)S(1)}, u32[]{:S(2)}, u32[]{:S(2)}) collective-permute-start(f32[16,512]{1,0:T(8,128)S(1)} %get-tuple-element.7), channel_id=1, source_target_pairs={{0,1},{1,2},{2,3},{3,4},{4,5},{5,6},{6,7},{7,8},{8,9},{9,10},{10,1... | collective-permute-start | bytes 98312 | tf_op jit(solution)/shard_map/ppermute | solution.py:408
  8.3 2.5 %copy-start.2 = (s32[32]{0:T(128)}, s32[32]{0:T(128)S(1)}, u32[]{:S(2)}) copy-start(s32[32]{0:T(128)S(1)} %compare_select_fusion.perm_ref) | copy-start | bytes 388
  10.8 0.6 copy-start
  11.5 0.6 copy-start.1

commit v3 on v0

v3 whole, which is shorter than its diff:
```python
import functools

import jax
import jax.numpy as jnp
from jax import lax
from jax.experimental import pallas as pl
from jax.experimental.pallas import tpu as pltpu
from jax.sharding import PartitionSpec as P

F32 = jnp.float32
BF16 = jnp.bfloat16


def halves(x):
    high = x.astype(BF16)
    return high, (x - high.astype(F32)).astype(BF16)


def factor_kernel(block, scale, g_ref, r_ref, m_ref, a_ref):
    size = a_ref.shape[0]
    hi = lax.Precision.HIGHEST
    a_ref[...] = jnp.zeros_like(a_ref)
    for q, (i, j) in enumerate(upper_blocks(size // block)):
        depth = block // 8
        part = g_ref[q * depth : (q + 1) * depth].reshape(block, block)
        a_ref[i * block : (i + 1) * block, j * block : (j + 1) * block] = part * scale
    tiles_count = block // 8
    eye_row = lax.broadcasted_iota(jnp.int32, (8, block), 0)
    eye_col = lax.broadcasted_iota(jnp.int32, (8, block), 1)
    step = 4

    def lane(value, k):
        return jnp.broadcast_to(value[:, k : k + 1], (8, block))

    def panel(p, carry):
        at = pl.multiple_of(p * block, block)
        left, right = [], []
        for t in range(tiles_count):
            left.append(a_ref[pl.ds(pl.multiple_of(at + 8 * t, 8), 8), pl.ds(at, block)])
            right.append((eye_row + 8 * t == eye_col).astype(F32))
        for k in range(0, block, step):
            home, top = divmod(k, 8)
            spread = lambda v, r: jnp.broadcast_to(v[r : r + 1, :], (8, block))
            rows_l = [spread(left[home], top + j) for j in range(step)]
            rows_r = [spread(right[home], top + j) for j in range(step)]
            corner = {(i, j): lane(rows_l[i], k + j) for i in range(step) for j in range(i, step)}
            inverse, link = [], {}
            for j in range(step):
                inverse.append(lax.rsqrt(corner[j, j]))
                for i in range(j + 1, step):
                    link[j, i] = corner[j, i] * inverse[j]
                for i in range(j + 1, step):
                    for h in range(i, step):
                        corner[i, h] = corner[i, h] - link[j, i] * link[j, h]

            def solve(values):
                done = []
                for j in range(step):
                    value = values[j]
                    for i in range(j):
                        value = value - link[i, j] * done[i]
                    done.append(value * inverse[j])
                return done

            rows_l, rows_r = solve(rows_l), solve(rows_r)
            for j in range(step):
                m_ref[k + j : k + j + 1, :] = rows_r[j][0:1, :]
            first = home if top + step < 8 else home + 1
            for t in range(first, tiles_count):
                columns = solve([lane(left[t], k + j) for j in range(step)])
                for j in range(step):
                    column = columns[j]
                    if t == home:
                        column = jnp.where(eye_row >= top + step, column, 0.0)
                    left[t] = left[t] - column * rows_l[j]
                    right[t] = right[t] - column * rows_r[j]
        rows = lax.dot_general(
            m_ref[...], a_ref[pl.ds(at, block), :], (((1,), (0,)), ((), ())),
            precision=hi, preferred_element_type=F32,
        )
        keep = lax.broadcasted_iota(jnp.int32, rows.shape, 1) >= (
            lax.broadcasted_iota(jnp.int32, rows.shape, 0) + at
        )
        rows = jnp.where(keep, rows, 0.0)
        r_ref[pl.ds(at, block), :] = rows

        @pl.when(p < size // block - 1)
        def _():
            a_ref[...] -= lax.dot_general(
                rows, rows, (((0,), (0,)), ((), ())),
                precision=hi, preferred_element_type=F32,
            )
        return carry

    lax.fori_loop(0, size // block, panel, 0)


BLOCK = 128


def upper_blocks(count):
    return [(i, j) for i in range(count) for j in range(i, count)]


def factor(packed, size, sample_count):
    return pl.pallas_call(
        functools.partial(factor_kernel, BLOCK, 1.0 / sample_count),
        out_shape=jax.ShapeDtypeStruct((size, size), F32),
        in_specs=[pl.BlockSpec(memory_space=pltpu.VMEM)],
        out_specs=pl.BlockSpec(memory_space=pltpu.VMEM),
        scratch_shapes=[pltpu.VMEM((BLOCK, BLOCK), F32), pltpu.VMEM((size, size), F32)],
        name="factor",
    )(packed)


PIECES = 4
FIR = 128


def sketch_kernel(tm, grp, scale, copies_of, taps_ref, series_ref, flips_ref, owner_ref,
                  sk_ref, gram_ref, x_ref, halo, x_high, x_low, t_high, t_low, h_ref, y_ref,
                  held, sums, part, *scratch):
    tm_bits, grp_bits = tm.bit_length() - 1, grp.bit_length() - 1
    stages = tm_bits + grp_bits
    devices = tm * grp
    groups = gram_groups(tm_bits, grp_bits)
    arrived, landed = scratch[:PIECES * stages], scratch[PIECES * stages : -3]
    local_sem, send_sem, recv_sem = scratch[-3:]
    t, g = lax.axis_index("tm"), lax.axis_index("grp")
    core = t % 2
    rows, width = x_ref.shape[1], x_ref.shape[2]
    half = halo.shape[1]
    per_device = held.shape[2]
    tap_count = taps_ref.shape[0]
    order = h_ref.shape[0]

    even, odd = stage_bits(tm, grp)
    mix = lambda u, v: u * (1 - core) + v * core

    def own_bit(bit):
        return (t // 2 ** (bit - grp_bits)) % 2 if bit >= grp_bits else (g // 2**bit) % 2

    values, deltas = [], []
    for label in range(stages):
        moves = []
        for bit in (even[label], odd[label]):
            value = own_bit(bit)
            if bit >= grp_bits:
                moves.append((value, (1 - 2 * value) * 2 ** (bit - grp_bits), 0))
            else:
                moves.append((value, 0, (1 - 2 * value) * 2**bit))
        if even[label] == odd[label]:
            value, dt, dg = moves[0]
        else:
            value, dt, dg = (mix(u, v) for u, v in zip(*moves))
        values.append(value)
        deltas.append((dt, dg))

    def peer(labels):
        pt, pg = t, g
        for label in labels:
            pt, pg = pt + deltas[label][0], pg + deltas[label][1]
        return pt, pg

    linear = t * grp + g
    after = (linear + 1) % devices
    before = (linear + devices - 1) % devices
    after, before = (after // grp, after % grp), (before // grp, before % grp)
    greeted = [peer([label]) for label in range(stages)]
    greeted += [peer(pair) for pair in groups if len(pair) > 1] + [after, before]
    barrier = pltpu.get_barrier_semaphore()
    mesh_ids = pl.DeviceIdType.MESH

    def load(c):
        return pltpu.make_async_copy(
            series_ref.at[:, pl.ds(c * width, width)], x_ref.at[c % 2], local_sem.at[c % 2])

    load(0).start()
    for who in greeted:
        pl.semaphore_signal(barrier, inc=1, device_id=who, device_id_type=mesh_ids)
    pl.semaphore_wait(barrier, len(greeted))

    def remote(source, target, slot, who):
        return pltpu.make_async_remote_copy(
            src_ref=source, dst_ref=target, send_sem=send_sem.at[slot],
            recv_sem=recv_sem.at[slot], device_id=who, device_id_type=mesh_ids)

    halo_low = remote(series_ref.at[pl.ds(rows - half, half), :], halo.at[0], 0, after)
    halo_high = remote(series_ref.at[pl.ds(0, half), :], halo.at[1], 1, before)
    halo_low.start()
    halo_high.start()

    lag = lax.broadcasted_iota(jnp.int32, t_high.shape, 1) - lax.broadcasted_iota(
        jnp.int32, t_high.shape, 0)
    band = jnp.zeros(t_high.shape, F32)
    for k in range(tap_count):
        band = jnp.where(lag == k, taps_ref[k], band)
    t_high[...], t_low[...] = halves(band)
    parity = lax.broadcasted_iota(jnp.int32, (order, order), 0) & lax.broadcasted_iota(
        jnp.int32, (order, order), 1)
    for shift in (4, 2, 1):
        parity = parity ^ (parity >> shift)
    h_ref[...] = (1 - 2 * (parity & 1)).astype(F32)
    halo_low.wait_recv()
    halo_high.wait_recv()

    order_of = [list(range(stages))] * PIECES
    order_of[0] = [0] + list(range(tm_bits, stages)) + list(range(1, tm_bits))

    def slab_of(d, c):
        bits = odd if (d >> grp_bits) & 1 else even
        slab = 0
        for label in order_of[c]:
            bit = bits[label]
            value = own_bit(bit)
            slab = slab * 2 + ((1 - value) if (d >> bit) & 1 else value)
        return slab

    def dot(u, v):
        return jnp.dot(u, v, preferred_element_type=F32)

    first_rows = (linear > 0).astype(F32)
    last_rows = (linear < devices - 1).astype(F32)
    hadamards = rows // order
    tile = 8

    def produce(c):
        load(c).wait()
        if c + 1 < PIECES:
            load(c + 1).start()
        lanes = slice(c * width, (c + 1) * width)
        x_high[0:half, :], x_low[0:half, :] = halves(halo[0, :, lanes] * first_rows)
        x_high[half + rows :, :], x_low[half + rows :, :] = halves(halo[1, :, lanes] * last_rows)

        def split(i, carry):
            at = pl.multiple_of(i * order, order)
            high, low = halves(x_ref[c % 2, pl.ds(at, order), :])
            to = pl.multiple_of(at + half, half)
            x_high[pl.ds(to, order), :] = high
            x_low[pl.ds(to, order), :] = low
            return carry

        lax.fori_loop(0, hadamards, split, 0)

        def group(a, carry):
            parts = []
            for piece in range(order // FIR):
                at = pl.multiple_of(a * order + piece * FIR, FIR)
                high = x_high[pl.ds(at, FIR + 2 * half), :]
                low = x_low[pl.ds(at, FIR + 2 * half), :]
                parts.append(
                    dot(t_high[...], high) + (dot(t_high[...], low) + dot(t_low[...], high)))
            filtered = jnp.concatenate(parts, axis=0)
            signed = (h_ref[...] * flips_ref[pl.ds(a, 1), :].astype(F32)).astype(BF16)
            high, low = halves(filtered)
            y_ref[a] = dot(signed, high) + dot(signed, low)
            return carry

        lax.fori_loop(0, hadamards, group, 0)
        cut = order // per_device
        for strip in range(cut):
            slabs = [slab_of(a * cut + strip, c) for a in range(hadamards)]

            def butterfly(b, carry):
                row = pl.multiple_of(b * tile, tile)
                parts = [y_ref[a, pl.ds(strip * per_device + row, tile), :]
                         for a in range(hadamards)]
                step = 1
                while step < hadamards:
                    for i in range(hadamards):
                        if not i & step:
                            u, v = parts[i], parts[i + step]
                            parts[i], parts[i + step] = u + v, u - v
                    step *= 2
                for a in range(hadamards):
                    held[c, slabs[a], pl.ds(row, tile), :] = parts[a]
                return carry

            lax.fori_loop(0, per_device // tile, butterfly, 0)

    def owner_slot(s, c):
        slot = 0
        for place, label in enumerate(order_of[c]):
            if label == 0:
                continue
            bit = (s // 2 ** (stages - 1 - place)) % 2
            bit = bit + values[label] - 2 * bit * values[label]
            spots = [2 ** (b - 1 if b >= grp_bits else b) for b in (even[label], odd[label])]
            slot = slot + bit * (spots[0] if spots[0] == spots[1] else mix(*spots))
        return slot

    def sign(slot, k, bit):
        return (1 - 2 * ((owner_ref[slot, k] >> bit) & 1)).astype(F32)

    def combine(c, i):
        source = arrived[c * stages + i]

        def slab(s, carry):
            slot = owner_slot(s, c)
            for k in range(copies_of):
                value = sign(slot, k, order_of[c][i])
                if i == 0:
                    sums[c, s, k] = held[c, s] + value * source[s]
                else:
                    sums[c, s, k] = sums[c, s, k] + value * source[s, k]
            return carry

        lax.fori_loop(0, devices >> (i + 1), slab, 0)

    copies = {}

    def send(c, i):
        count = devices >> (i + 1)
        whole = held if i == 0 else sums
        copies[c, i] = remote(whole.at[c, pl.ds(count, count)], arrived[c * stages + i],
                              2 + c * stages + i, peer([order_of[c][i]]))
        copies[c, i].start()

    def finish(c, i):
        copies[c, i].wait_recv()
        combine(c, i)
        if i + 1 < stages:
            send(c, i + 1)
        else:
            slot = owner_slot(0, c)
            for k in range(copies_of):
                sk_ref[k, :, c * width : (c + 1) * width] = (
                    sums[c, 0, k] * (sign(slot, k, stages) * scale))

    for c in range(PIECES):
        produce(c)
        send(c, 0)
        if c:
            finish(c - 1, 0)
    finish(PIECES - 1, 0)

    def due(c, i):
        return (8 + 6 * i if c else 11 + 10 * i) + 8 * c * (c > 0) + (i if c == 0 else 0)

    later = [(c, i) for c in range(PIECES) for i in range(1, stages)]
    for c, i in sorted(later, key=lambda ci: (due(*ci), ci[1])):
        finish(c, i)

    blocks = sk_ref.shape[2] // BLOCK
    depth = BLOCK // 8
    total = part.shape[0]
    sketch = sk_ref[...].reshape(copies_of * per_device, sk_ref.shape[2])
    q = 0
    for i in range(blocks):
        product = lax.dot_general(
            sketch[:, i * BLOCK : (i + 1) * BLOCK], sketch[:, i * BLOCK :],
            (((0,), (0,)), ((), ())),
            precision=lax.Precision.HIGHEST, preferred_element_type=F32)
        for j in range(blocks - i):
            part[q * depth : (q + 1) * depth] = product[:, j * BLOCK : (j + 1) * BLOCK].reshape(
                depth, 8, BLOCK)
            q += 1
    if q * depth < total:
        part[q * depth :] = jnp.zeros((total - q * depth, 8, BLOCK), F32)

    slot = 2 + PIECES * stages
    offset, size = 0, total
    plan = []
    for n, labels in enumerate(groups):
        ways = 2 ** len(labels)
        size //= ways
        flight = []
        for r in range(1, ways):
            chosen = [label for p, label in enumerate(labels) if (r >> p) & 1]
            seg = 0
            for label in labels:
                value = values[label]
                seg = seg * 2 + ((1 - value) if label in chosen else value)
            copy = remote(part.at[pl.ds(offset + seg * size, size)], landed[n].at[r - 1],
                          slot, peer(chosen))
            slot += 1
            copy.start()
            flight.append(copy)
            plan.append(copy)
        seg = 0
        for label in labels:
            seg = seg * 2 + values[label]
        offset = offset + seg * size
        total_here = part[pl.ds(offset, size)]
        for r, copy in enumerate(flight):
            copy.wait_recv()
            total_here = total_here + landed[n][r]
        target = part if n + 1 < len(groups) else gram_ref
        target[pl.ds(offset, size)] = total_here
    for labels in reversed(groups):
        ways = 2 ** len(labels)
        span = pl.ds(offset, size)
        flight = []
        for r in range(1, ways):
            chosen = [label for p, label in enumerate(labels) if (r >> p) & 1]
            copy = remote(gram_ref.at[span], gram_ref.at[span], slot, peer(chosen))
            slot += 1
            copy.start()
            flight.append(copy)
            plan.append(copy)
        for copy in flight:
            copy.wait_recv()
        seg = 0
        for label in labels:
            seg = seg * 2 + values[label]
        offset = offset - seg * size
        size *= ways
    halo_low.wait_send()
    halo_high.wait_send()
    for copy in list(copies.values()) + plan:
        copy.wait_send()


def gram_groups(tm_bits, grp_bits):
    def pairs(labels):
        return [labels[i : i + 2] for i in range(0, len(labels), 2)]

    return [[0]] + pairs(list(range(1, tm_bits))) + pairs(
        list(range(tm_bits, tm_bits + grp_bits)))


def sketch_and_gram(tm, grp, scale, copies_of, taps, series, flips, owners):
    rows, columns = series.shape
    devices = tm * grp
    half = (taps.shape[0] - 1) // 2
    per_device = rows // devices
    width = columns // PIECES
    order = flips.shape[1]
    stages = devices.bit_length() - 1
    groups = gram_groups(tm.bit_length() - 1, grp.bit_length() - 1)
    blocks = columns // BLOCK
    needed = blocks * (blocks + 1) // 2 * (BLOCK // 8)
    total = -(-needed // devices) * devices
    arrived = []
    for _ in range(PIECES):
        arrived.append(pltpu.VMEM((devices // 2, per_device, width), F32))
        for i in range(1, stages):
            arrived.append(pltpu.VMEM((devices >> (i + 1), copies_of, per_device, width), F32))
    landed, size, hops = [], total, 0
    for labels in groups:
        size >>= len(labels)
        hops += 2 ** len(labels) - 1
        landed.append(pltpu.VMEM((2 ** len(labels) - 1, size, 8, BLOCK), F32))
    slots = 2 + PIECES * stages + 2 * hops
    sem = pltpu.SemaphoreType.DMA
    vmem = pl.BlockSpec(memory_space=pltpu.VMEM)
    return pl.pallas_call(
        functools.partial(sketch_kernel, tm, grp, scale, copies_of),
        out_shape=(jax.ShapeDtypeStruct((copies_of, per_device, columns), F32),
                   jax.ShapeDtypeStruct((total, 8, BLOCK), F32)),
        in_specs=[pl.BlockSpec(memory_space=pltpu.SMEM), pl.BlockSpec(memory_space=pl.ANY),
                  vmem, vmem],
        out_specs=(vmem, vmem),
        scratch_shapes=[
            pltpu.VMEM((2, rows, width), F32),
            pltpu.VMEM((2, half, columns), F32),
            pltpu.VMEM((rows + 2 * half, width), BF16),
            pltpu.VMEM((rows + 2 * half, width), BF16),
            pltpu.VMEM((FIR, FIR + 2 * half), BF16),
            pltpu.VMEM((FIR, FIR + 2 * half), BF16),
            pltpu.VMEM((order, order), F32),
            pltpu.VMEM((rows // order, order, width), F32),
            pltpu.VMEM((PIECES, devices, per_device, width), F32),
            pltpu.VMEM((PIECES, devices // 2, copies_of, per_device, width), F32),
            pltpu.VMEM((total, 8, BLOCK), F32),
            *arrived, *landed, sem((2,)), sem((slots,)), sem((slots,)),
        ],
        compiler_params=pltpu.CompilerParams(
            collective_id=0, has_side_effects=True, vmem_limit_bytes=60 * 2**20),
        name="sketch",
    )(taps, series, flips, owners)


def stage_bits(tm, grp):
    grp_bits = list(range(grp.bit_length() - 1))
    base = len(grp_bits)
    tm_bits = list(range(base, base + tm.bit_length() - 1))
    core, rest = tm_bits[:1], tm_bits[1:]
    near, far = rest[: len(rest) // 2], rest[len(rest) // 2 :]
    return core + near + far + grp_bits, core + far + near + grp_bits


def bit_parity(value, bits):
    parity = jnp.zeros_like(value)
    for bit in range(bits):
        parity = parity ^ (value >> bit & 1)
    return parity


def on_device(series, filter_taps, sign_flips, samples):
    rows_dev, columns = series.shape
    tm, grp = lax.axis_size("tm"), lax.axis_size("grp")
    devices = tm * grp
    sample_count = samples.shape[0]
    per_device = rows_dev // devices
    copies = sample_count // rows_dev
    core = lax.axis_index("tm") % 2
    me = lax.axis_index("tm") * grp + lax.axis_index("grp")
    even, odd = stage_bits(tm, grp)
    order = min(256, rows_dev)

    owner = (samples // rows_dev).reshape(tm // 2, 2, grp, per_device, copies)
    owner = lax.dynamic_index_in_dim(owner, core, 1, keepdims=False)
    owner = owner.reshape(devices // 2, per_device, copies).transpose(0, 2, 1)
    code = jnp.zeros_like(owner)
    for stage, (even_bit, odd_bit) in enumerate(zip(even, odd)):
        code = code + ((owner >> jnp.where(core == 0, even_bit, odd_bit) & 1) << stage)
    code = code + (bit_parity(owner & me, devices.bit_length()) << len(even))
    codes = jnp.broadcast_to(code[..., None], code.shape + (columns // PIECES,))
    sums, packed = sketch_and_gram(
        tm, grp, (rows_dev * devices) ** -0.5, copies, filter_taps, series,
        sign_flips.reshape(rows_dev // order, order), codes)
    sketch = sums.transpose(1, 0, 2).reshape(-1, columns)
    return sketch, factor(packed, columns, sample_count)


def solution(mesh):
    return jax.shard_map(
        on_device,
        mesh=mesh,
        in_specs=(P(("tm", "grp"), None), P(), P(("tm", "grp")), P()),
        out_specs=(P(("tm", "grp"), None), P()),
        check_vma=False,
    )
```

time: 664 us -> 174 us (0.26)
  waiting for transfers between devices: 315 us -> 0 us
  other arithmetic: 212 us -> 0.83 us
  Pallas kernels: 0 us -> 164 us
  matrix products: 47 us -> 0 us
  local copies, waits for them, and re-layouts: 54.7 us -> 8.18 us
  between operations: 17.3 us -> 0.71 us
  starting transfers between devices: 13.3 us -> 0 us
    all_to_all x1 -> x0, waiting for transfers between devices: 181 us -> none  [on_device(): lax.all_to_all(outgoing, ('tm', 'grp'), split_axis=0, concat_axis=0, tile...]
    pallas_call x0 -> x2, Pallas kernels: none -> 164 us  [the longest x1 136 us: sketch_and_gram(): pl.pallas_call(functools.partial(sketch_kernel, tm, grp, scale, copies_of...]
    psum x1 -> x0, waiting for transfers between devices: 135 us -> none  [on_device(): gram = lax.psum(local_gram, ('tm', 'grp'))]
    mul x1 -> x0, other arithmetic: 123 us -> none  [on_device(): flipped = filtered * sign_flips.astype(jnp.float32)[:, None]]
    another operation x14 -> x0, other arithmetic: 78.8 us -> none  [on_device(): lower = jnp.linalg.cholesky(gram / sample_count)]
    dot_general x4 -> x0, matrix products: 45.1 us -> none  [the longest x1 16.9 us: on_device(): jnp.einsum('op,pkw->okw', hadamard(devices_all), stacked, precision=lax.P...]
    gather x2 -> x0, local copies, waits for them, and re-layouts: 26 us -> none  [the longest x1 21.4 us: on_device(): outgoing = jnp.take(mixed, used_positions, axis=0)]
    concatenate x2 -> x0, local copies, waits for them, and re-layouts: 12.1 us -> none  [extended(): block = jnp.concatenate([low, block, high], axis=dim)]
  transfers between devices with their start and end apart: 4 -> 0, of which waited for: 2 -> 0; matrix products, arithmetic and copies ran while one was open for 3% -> 0% of each run, Pallas kernels for 0% -> 0%
where the time goes in v3:
time: 174 us
  Pallas kernels  164 us (94%)
  local copies, waits for them, and re-layouts  8.18 us (5%)
    pallas_call x1, Pallas kernels, sketch_and_gram(): pl.pallas_call(functools.partial(sketch_kernel, tm, grp, scale, copies_of...  136 us
    pallas_call x1, Pallas kernels, factor(): pl.pallas_call(functools.partial(factor_kernel, BLOCK, 1.0 / sample_count...  28.8 us

profile of v3, /device:TPU:0, one launch (start us, length us, event | category | flops | bytes accessed | tf_op | source)
XLA Modules:
  0.0 174.1 jit_solution(7476308762035625984)
XLA Ops:
  0.7 1.3 reshape.72.flips_ref
  2.0 0.8 add_select_fusion
  2.8 2.1 %reshape.73 = s32[4,2,4,128,2]{4,3,2,1,0:T(8,128)S(1)} reshape(s32[8192]{0:T(1024)S(1)} %add_select_fusion) | data formatting | bytes 65536 | tf_op jit(solution)/shard_map/reshape | solution.py:502
  4.9 0.1 constant_dynamic-slice_fusion
  5.0 0.3 copy.14
  5.3 0.1 shift-left_add_fusion
  5.4 1.7 broadcast_in_dim.2.owner_ref
  7.1 135.5 %sketch.1 = (f32[2,128,512]{2,1,0:T(8,128)}, f32[160,8,128]{2,1,0:T(8,128)}) custom-call(f32[33]{0:T(128)} %taps_ref.1, f32[4096,512]{1,0:T(8,128)} %series_ref.1, s32[16,256]{1,0:T(8,128)} %reshape.72.flips_ref, s32[16,2,128,128]{3,2,1,0:T(8,128)} %broadcast_in_dim.2.owner_ref), custom_call_target="tpu_custom_call" | custom-call | tf_op jit(solution)/shard_map/sketch/pallas_call | solution.py:447
  142.6 1.4 copy.13
  144.1 1.2 reshape.74
  145.2 28.8 %factor.1 = f32[512,512]{1,0:T(8,128)} custom-call(f32[160,8,128]{2,1,0:T(8,128)} %get-tuple-element.5.g_ref), custom_call_target="tpu_custom_call" | custom-call | tf_op jit(solution)/shard_map/factor/pallas_call | solution.py:106
  (2 shorter events, 0.0 us)

commit v4 on v3

--- a/solution.py
+++ b/solution.py
@@ -27,7 +27,7 @@
     tiles_count = block // 8
     eye_row = lax.broadcasted_iota(jnp.int32, (8, block), 0)
     eye_col = lax.broadcasted_iota(jnp.int32, (8, block), 1)
-    step = 4
+    step = 8
 
     def lane(value, k):
         return jnp.broadcast_to(value[:, k : k + 1], (8, block))
@@ -114,6 +114,8 @@
 
 
 PIECES = 4
+PARTS = 2
+UNITS = PIECES * PARTS
 FIR = 128
 
 
@@ -124,7 +126,7 @@
     stages = tm_bits + grp_bits
     devices = tm * grp
     groups = gram_groups(tm_bits, grp_bits)
-    arrived, landed = scratch[:PIECES * stages], scratch[PIECES * stages : -3]
+    arrived, landed = scratch[:UNITS * stages], scratch[UNITS * stages : -3]
     local_sem, send_sem, recv_sem = scratch[-3:]
     t, g = lax.axis_index("tm"), lax.axis_index("grp")
     core = t % 2
@@ -289,57 +291,73 @@
             slot = slot + bit * (spots[0] if spots[0] == spots[1] else mix(*spots))
         return slot
 
-    def sign(slot, k, bit):
-        return (1 - 2 * ((owner_ref[slot, k] >> bit) & 1)).astype(F32)
-
-    def combine(c, i):
-        source = arrived[c * stages + i]
+    depth_of = per_device // PARTS
+
+    def strip_of(unit):
+        at = unit % PARTS * depth_of
+        return unit // PARTS, slice(at, at + depth_of)
+
+    def sign(slot, k, span, bit):
+        return (1 - 2 * ((owner_ref[slot, k, span] >> bit) & 1)).astype(F32)
+
+    def combine(unit, i):
+        c, span = strip_of(unit)
+        source = arrived[unit * stages + i]
 
         def slab(s, carry):
             slot = owner_slot(s, c)
             for k in range(copies_of):
-                value = sign(slot, k, order_of[c][i])
+                value = sign(slot, k, span, order_of[c][i])
                 if i == 0:
-                    sums[c, s, k] = held[c, s] + value * source[s]
+                    sums[unit, s, k] = held[c, s, span] + value * source[s]
                 else:
-                    sums[c, s, k] = sums[c, s, k] + value * source[s, k]
+                    sums[unit, s, k] = sums[unit, s, k] + value * source[s, k]
             return carry
 
         lax.fori_loop(0, devices >> (i + 1), slab, 0)
 
     copies = {}
 
-    def send(c, i):
+    def send(unit, i):
+        c, span = strip_of(unit)
         count = devices >> (i + 1)
-        whole = held if i == 0 else sums
-        copies[c, i] = remote(whole.at[c, pl.ds(count, count)], arrived[c * stages + i],
-                              2 + c * stages + i, peer([order_of[c][i]]))
-        copies[c, i].start()
-
-    def finish(c, i):
-        copies[c, i].wait_recv()
-        combine(c, i)
+        if i == 0:
+            source = held.at[c, pl.ds(count, count), pl.ds(span.start, depth_of), :]
+        else:
+            source = sums.at[unit, pl.ds(count, count)]
+        copies[unit, i] = remote(source, arrived[unit * stages + i],
+                                 2 + unit * stages + i, peer([order_of[c][i]]))
+        copies[unit, i].start()
+
+    def finish(unit, i):
+        c, span = strip_of(unit)
+        copies[unit, i].wait_recv()
+        combine(unit, i)
         if i + 1 < stages:
-            send(c, i + 1)
+            send(unit, i + 1)
         else:
             slot = owner_slot(0, c)
             for k in range(copies_of):
-                sk_ref[k, :, c * width : (c + 1) * width] = (
-                    sums[c, 0, k] * (sign(slot, k, stages) * scale))
+                sk_ref[k, span, c * width : (c + 1) * width] = (
+                    sums[unit, 0, k] * (sign(slot, k, span, stages) * scale))
 
     for c in range(PIECES):
         produce(c)
-        send(c, 0)
-        if c:
-            finish(c - 1, 0)
-    finish(PIECES - 1, 0)
-
-    def due(c, i):
-        return (8 + 6 * i if c else 11 + 10 * i) + 8 * c * (c > 0) + (i if c == 0 else 0)
-
-    later = [(c, i) for c in range(PIECES) for i in range(1, stages)]
-    for c, i in sorted(later, key=lambda ci: (due(*ci), ci[1])):
-        finish(c, i)
+        for p in range(PARTS):
+            send(c * PARTS + p, 0)
+        for p in range(PARTS):
+            if c:
+                finish((c - 1) * PARTS + p, 0)
+    for p in range(PARTS):
+        finish((PIECES - 1) * PARTS + p, 0)
+
+    def due(unit, i):
+        c, p = unit // PARTS, unit % PARTS / PARTS
+        return 8 + 4 * i + 8 * (c + p) if c else 11 + 7 * i + 11 * p
+
+    later = [(u, i) for u in range(UNITS) for i in range(1, stages)]
+    for u, i in sorted(later, key=lambda ui: (due(*ui), ui[1])):
+        finish(u, i)
 
     blocks = sk_ref.shape[2] // BLOCK
     depth = BLOCK // 8
@@ -358,7 +376,7 @@
     if q * depth < total:
         part[q * depth :] = jnp.zeros((total - q * depth, 8, BLOCK), F32)
 
-    slot = 2 + PIECES * stages
+    slot = 2 + UNITS * stages
     offset, size = 0, total
     plan = []
     for n, labels in enumerate(groups):
@@ -432,16 +450,17 @@
     needed = blocks * (blocks + 1) // 2 * (BLOCK // 8)
     total = -(-needed // devices) * devices
     arrived = []
-    for _ in range(PIECES):
-        arrived.append(pltpu.VMEM((devices // 2, per_device, width), F32))
+    thin = per_device // PARTS
+    for _ in range(UNITS):
+        arrived.append(pltpu.VMEM((devices // 2, thin, width), F32))
         for i in range(1, stages):
-            arrived.append(pltpu.VMEM((devices >> (i + 1), copies_of, per_device, width), F32))
+            arrived.append(pltpu.VMEM((devices >> (i + 1), copies_of, thin, width), F32))
     landed, size, hops = [], total, 0
     for labels in groups:
         size >>= len(labels)
         hops += 2 ** len(labels) - 1
         landed.append(pltpu.VMEM((2 ** len(labels) - 1, size, 8, BLOCK), F32))
-    slots = 2 + PIECES * stages + 2 * hops
+    slots = 2 + UNITS * stages + 2 * hops
     sem = pltpu.SemaphoreType.DMA
     vmem = pl.BlockSpec(memory_space=pltpu.VMEM)
     return pl.pallas_call(
@@ -461,7 +480,7 @@
             pltpu.VMEM((order, order), F32),
             pltpu.VMEM((rows // order, order, width), F32),
             pltpu.VMEM((PIECES, devices, per_device, width), F32),
-            pltpu.VMEM((PIECES, devices // 2, copies_of, per_device, width), F32),
+            pltpu.VMEM((UNITS, devices // 2, copies_of, thin, width), F32),
             pltpu.VMEM((total, 8, BLOCK), F32),
             *arrived, *landed, sem((2,)), sem((slots,)), sem((slots,)),
         ],

time: 174 us -> 167 us (0.960)
  Pallas kernels: 164 us -> 157 us
    pallas_call x1, Pallas kernels: 28.8 us -> 24.3 us  [factor(): pl.pallas_call(functools.partial(factor_kernel, BLOCK, 1.0 / sample_count...]
    pallas_call x1, Pallas kernels: 136 us -> 133 us  [sketch_and_gram(): pl.pallas_call(functools.partial(sketch_kernel, tm, grp, scale, copies_of...]
where the time goes in v4:
time: 167 us
  Pallas kernels  157 us (94%)
  local copies, waits for them, and re-layouts  8.18 us (5%)
    pallas_call x1, Pallas kernels, sketch_and_gram(): pl.pallas_call(functools.partial(sketch_kernel, tm, grp, scale, copies_of...  133 us
    pallas_call x1, Pallas kernels, factor(): pl.pallas_call(functools.partial(factor_kernel, BLOCK, 1.0 / sample_count...  24.3 us

profile of v4, /device:TPU:0, one launch (start us, length us, event | category | flops | bytes accessed | tf_op | source)
XLA Modules:
  0.0 166.9 jit_solution(7555952402020279507)
XLA Ops:
  0.7 1.3 reshape.72.flips_ref
  2.0 0.8 add_select_fusion
  2.8 2.1 %reshape.73 = s32[4,2,4,128,2]{4,3,2,1,0:T(8,128)S(1)} reshape(s32[8192]{0:T(1024)S(1)} %add_select_fusion) | data formatting | bytes 65536 | tf_op jit(solution)/shard_map/reshape | solution.py:521
  4.9 0.1 constant_dynamic-slice_fusion
  5.0 0.3 copy.14
  5.3 0.1 shift-left_add_fusion
  5.4 1.7 %broadcast_in_dim.2.owner_ref = s32[16,2,128,128]{3,2,1,0:T(8,128)} broadcast(s32[16,2,128]{2,1,0:T(2,128)S(1)} %copy.12), dimensions={0,1,2} | broadcast | bytes 2113536 | tf_op jit(solution)/shard_map/broadcast_in_dim | solution.py:528
  7.1 132.9 %sketch.1 = (f32[2,128,512]{2,1,0:T(8,128)}, f32[160,8,128]{2,1,0:T(8,128)}) custom-call(f32[33]{0:T(128)} %taps_ref.1, f32[4096,512]{1,0:T(8,128)} %series_ref.1, s32[16,256]{1,0:T(8,128)} %reshape.72.flips_ref, s32[16,2,128,128]{3,2,1,0:T(8,128)} %broadcast_in_dim.2.owner_ref), custom_call_target="tpu_custom_call" | custom-call | tf_op jit(solution)/shard_map/sketch/pallas_call | solution.py:466
  140.0 1.4 copy.13
  141.5 1.2 reshape.74
  142.6 24.3 %factor.1 = f32[512,512]{1,0:T(8,128)} custom-call(f32[160,8,128]{2,1,0:T(8,128)} %get-tuple-element.5.g_ref), custom_call_target="tpu_custom_call" | custom-call | tf_op jit(solution)/shard_map/factor/pallas_call | solution.py:106
  (2 shorter events, 0.0 us)
